TPU v7x, 32 devices: a whole 2x2x4 slice. The times are simulated.
32 devices in a mesh: space: 8 (over z, y), scen: 4 (over x, core).
Axes of the slice: x: 2, y: 2, z: 4, core: 2. Of those that a mesh axis runs over, the one named last changes fastest.
Arguments:
- start_fraction: bfloat16 [16, 24, 16384], P('scen', None, 'space'), may hold values from 0 to 1
- ore_value: bfloat16 [16, 24, 16384], P('scen', None, 'space'), may hold values from -6 to 6
- dual_price: float32 [16, 24, 16384], P('scen', None, 'space'), may hold values from -3 to 3
- patterns: bfloat16 [3, 512, 512], replicated, may hold values from -0.15625 to 0.15625
- cone_list: int32 [32, 3], P('space'), may hold values from 0 to 31, as said below
- node_list: int32 [2, 16], replicated, may hold values from 0 to 15, as said below
- probability: float32 [16], replicated, may hold values from 0.5 to 2
Outputs:
- fraction: float32 [16, 24, 16384], P('scen', None, 'space')
- dual_out: float32 [16, 24, 16384], P('scen', None, 'space')
Inputs may be any that keep to these rules, and one draw needn't show every extreme that they name: `cone_list`: row i holds i, then tile i - 1 and tile i + 1 in an order drawn per tile; where a neighbour lies outside the slab the tile itself stands in its place. `node_list`: row 0 holds second-section nodes below 4, row 1 third-section nodes; every node holds a scenario, and scenarios that share a third-section node share their second-section node.
All inputs are finite; a program needn't handle non-finite values.
Results may differ from a plain program's by a relative error of at most 0.00079.
Values may be sent and summed in bfloat16 or wider, within the bound.
No kernel may reach another device: no remote copies, remote signals or barrier semaphores. Data moves between devices by JAX's collectives and lax.ppermute only.
A program may use at most 64 MiB of HBM per device.

v0:
```python
import jax
import jax.numpy as jnp
from jax import lax
from jax.sharding import PartitionSpec as P

TILE = 512
SECTIONS = 4
NODES1 = 4
NODES2 = 16
ITERS = 2
PG_STEPS = 2


def extended_2(array, sides, width):
    for axis, dim in sides:
        size, length = (lax.axis_size(axis), array.shape[dim])
        up = [(i, (i + 1) % size) for i in range(size - 1)]
        down = [(j, i) for i, j in up]
        last = lax.slice_in_dim(array, length - width, length, axis=dim)
        first = lax.slice_in_dim(array, 0, width, axis=dim)
        before = lax.ppermute(last, axis, up)
        after = lax.ppermute(first, axis, down)
        array = jnp.concatenate([before, array, after], axis=dim)
    return array


def node_weights(nodes, weights_in, count):
    return (nodes[:, None] == jnp.arange(count)[None, :]).astype(jnp.float32) * weights_in[:, None]


def tree_center(fraction, node_list, probability):
    quarter = fraction.shape[1] // SECTIONS
    scen_local = fraction.shape[0]
    leaf_part = fraction[:, (SECTIONS - 1) * quarter :]
    offset = lax.axis_index("scen") * scen_local
    local_prob = lax.dynamic_slice_in_dim(probability, offset, scen_local, 0)
    local_nodes = lax.dynamic_slice_in_dim(node_list, offset, scen_local, 1)
    weight_one = node_weights(local_nodes[0], local_prob, NODES1)
    weight_two = node_weights(local_nodes[1], local_prob, NODES2)
    root_term = jnp.tensordot(
        local_prob, fraction[:, :quarter], axes=1, precision=lax.Precision.HIGHEST
    )
    first_term = jnp.tensordot(
        weight_one,
        fraction[:, quarter : 2 * quarter],
        axes=((0,), (0,)),
        precision=lax.Precision.HIGHEST,
    )
    second_term = jnp.tensordot(
        weight_two,
        fraction[:, 2 * quarter : 3 * quarter],
        axes=((0,), (0,)),
        precision=lax.Precision.HIGHEST,
    )
    root_sum, first_sum, second_sum = lax.psum((root_term, first_term, second_term), "scen")
    full_one = node_weights(node_list[0], probability, NODES1)
    full_two = node_weights(node_list[1], probability, NODES2)
    root_mean = root_sum / jnp.sum(probability)
    first_mean = first_sum / jnp.sum(full_one, axis=0)[:, None, None]
    second_mean = second_sum / jnp.sum(full_two, axis=0)[:, None, None]
    root_part = jnp.broadcast_to(root_mean[None], (scen_local, quarter, fraction.shape[2]))
    first_part = jnp.take(first_mean, local_nodes[0], axis=0)
    second_part = jnp.take(second_mean, local_nodes[1], axis=0)
    return jnp.concatenate([root_part, first_part, second_part, leaf_part], axis=1)


def descend(fraction, ore_value, dual_now, center, local_cone, patterns):
    rounded = fraction.astype(jnp.bfloat16)
    full_shape = fraction.shape
    tile_view = rounded.reshape(full_shape[0], full_shape[1], full_shape[2] // TILE, TILE)
    extended = extended_2(tile_view, (("space", 2),), 1)
    accumulated = jnp.zeros((fraction.size // TILE, TILE), jnp.float32)
    for cone_slot in range(3):
        picked = jnp.take(extended, local_cone[:, cone_slot], axis=2).reshape(-1, TILE)
        accumulated = accumulated + jnp.dot(
            picked, patterns[cone_slot], preferred_element_type=jnp.float32
        )
    cone_mix = accumulated.reshape(full_shape)
    gradient = (
        -ore_value.astype(jnp.float32)
        + dual_now
        + 1.0 * (fraction - center)
        + 1.0 * (fraction - cone_mix)
    )
    return jnp.clip(fraction - 0.4 * gradient, 0.0, 1.0)


def body(start_fraction, ore_value, dual_price, patterns, cone_list, node_list, probability):
    first_tile = lax.axis_index("space") * cone_list.shape[0]
    local_cone = cone_list - first_tile + 1
    fraction = start_fraction.astype(jnp.float32)
    dual_now = dual_price
    center = tree_center(fraction, node_list, probability)
    for ph_round in range(ITERS):
        for inner_step in range(PG_STEPS):
            fraction = descend(fraction, ore_value, dual_now, center, local_cone, patterns)
        center = tree_center(fraction, node_list, probability)
        dual_now = dual_now + 1.0 * (fraction - center)
    return (fraction, dual_now)


def solution(mesh):
    in_specs = (
        P("scen", None, "space"),
        P("scen", None, "space"),
        P("scen", None, "space"),
        P(),
        P("space", None),
        P(),
        P(),
    )
    out_specs = (P("scen", None, "space"), P("scen", None, "space"))
    return jax.shard_map(body, mesh=mesh, in_specs=in_specs, out_specs=out_specs, check_vma=False)
```

profile of v0, /device:TPU:0, one launch (start us, length us, event | category | flops | bytes accessed | tf_op | source)
XLA Modules:
  0.0 301.8 jit_solution(3626839356143465838)
XLA Ops:
  8.3 4.9 %collective-permute-start = (bf16[4,24,1,512]{3,1,2,0:T(8,128)(2,1)S(1)}, bf16[4,24,1,512]{3,1,2,0:T(8,128)(2,1)S(1)}, u32[]{:S(2)}, u32[]{:S(2)}) collective-permute-start(bf16[4,24,1,512]{3,1,2,0:T(8,128)(2,1)S(1)} %get-tuple-element.41), channel_id=1, source_target_pairs={{0,4},{4,8},{8,12},{12,16},{16,20},{20,24},{24,28},{1,5},{5,9},{9,... | collective-permute-start | bytes 294920 | tf_op jit(solution)/shard_map/ppermute | solution.py:21
  20.8 12.4 %psum.63 = f32[6,2048]{1,0:T(8,128)S(1)} all-reduce(f32[6,2048]{1,0:T(8,128)S(1)} %bitcast.125), channel_id=1, replica_groups=mesh['space'=8,'scen'=4] {'scen'}, use_global_device_ids=true, to_apply=%region_0.0 | all-reduce | flops 12288 | bytes 98304 | tf_op jit(solution)/shard_map/psum | solution.py:55
  44.2 13.3 %all-reduce.11.cloned.1.call-done = (f32[16,6,2048]{2,0,1:T(8,128)}, f32[4,6,2048]{2,0,1:T(4,128)}) async-done(((f32[16,6,2048]{2,0,1:T(8,128)}, f32[4,6,2048]{2,0,1:T(4,128)}), (f32[16,6,2048]{2,0,1:T(8,128)}, f32[4,6,2048]{2,0,1:T(4,128)})) %all-reduce.11.cloned.1.call-update) | async-done | bytes 983056 | tf_op jit(solution)/shard_map/psum | solution.py:55
  61.3 2.6 gather_fusion.1
  69.5 3.9 %fusion.109 = (bf16[4,24,2048]{2,0,1:T(4,128)(2,1)}, f32[4,24,2048]{2,0,1:T(4,128)}) fusion(f32[4,24,2048]{2,1,0:T(8,128)} %reshape.94, f32[4,6,2048]{2,0,1:T(4,128)S(1)} %copy-done.14, f32[4,6,2048]{2,0,1:T(4,128)S(1)} %copy_select_fusion.4, f32[4,6,2048]{2,0,1:T(4,128)S(1)} %copy_select_fusion.5, f32[4,6,2048]{2,0,1:T(4,128)S(1)} %broadcast_in_dim.33, ...), kind=kLoop, calls=%fused_computation.216 | loop fusion | flops 2949120 | bytes 4325376 | tf_op jit(solution)/shard_map/convert_element_type | solution.py:68
  75.0 3.4 %collective-permute-start.2 = (bf16[4,24,1,512]{3,1,2,0:T(8,128)(2,1)S(1)}, bf16[4,24,1,512]{3,1,2,0:T(8,128)(2,1)S(1)}, u32[]{:S(2)}, u32[]{:S(2)}) collective-permute-start(bf16[4,24,1,512]{3,1,2,0:T(8,128)(2,1)S(1)} %copy.231), channel_id=1, source_target_pairs={{0,4},{4,8},{8,12},{12,16},{16,20},{20,24},{24,28},{1,5},{5,9},{9,... | collective-permute-start | bytes 294920 | tf_op jit(solution)/shard_map/ppermute | solution.py:21
  82.2 2.8 collective-permute-done.3
  89.8 2.5 gather_fusion.7
  104.6 3.9 %fusion.107 = (bf16[4,24,2048]{2,0,1:T(4,128)(2,1)}, f32[4,24,2048]{2,0,1:T(4,128)S(1)}) fusion(f32[4,24,2048]{2,0,1:T(4,128)} %get-tuple-element.27, f32[4,24,2048]{2,1,0:T(8,128)} %reshape.99, f32[4,6,2048]{2,0,1:T(4,128)} %slice.190, f32[4,6,2048]{2,0,1:T(4,128)} %copy-done.15, f32[4,6,2048]{2,0,1:T(4,128)} %copy-done.16, f32[4,6,2048]{2,0,1:T(4,128)} %copy-done.17, ...), kind=kLoop, calls=%fused_computation.215 | loop fusion | flops 2752512 | bytes 4718592 | tf_op jit(solution)/shard_map/convert_element_type | solution.py:68
  116.3 4.9 %collective-permute-start.4 = (bf16[4,24,1,512]{3,1,2,0:T(8,128)(2,1)}, bf16[4,24,1,512]{3,1,2,0:T(8,128)(2,1)}, u32[]{:S(2)}, u32[]{:S(2)}) collective-permute-start(bf16[4,24,1,512]{3,1,2,0:T(8,128)(2,1)} %copy.233), channel_id=1, source_target_pairs={{0,4},{4,8},{8,12},{12,16},{16,20},{20,24},{24,28},{1,5},{5,9},{9,... | collective-permute-start | bytes 294920 | tf_op jit(solution)/shard_map/ppermute | solution.py:21
  122.6 11.7 %psum.66 = f32[6,2048]{1,0:T(8,128)} all-reduce(f32[6,2048]{1,0:T(8,128)} %bitcast.126), channel_id=1, replica_groups=mesh['space'=8,'scen'=4] {'scen'}, use_global_device_ids=true, to_apply=%region_6.10 | all-reduce | flops 12288 | bytes 98304 | tf_op jit(solution)/shard_map/psum | solution.py:55
  148.9 2.5 gather_fusion.10
  153.8 2.5 gather_fusion.12
  175.0 3.2 %all-reduce.9.cloned.1.call-done = (f32[16,6,2048]{2,0,1:T(8,128)}, f32[4,6,2048]{2,0,1:T(4,128)}) async-done(((f32[16,6,2048]{2,0,1:T(8,128)}, f32[4,6,2048]{2,0,1:T(4,128)}), (f32[16,6,2048]{2,0,1:T(8,128)}, f32[4,6,2048]{2,0,1:T(4,128)})) %all-reduce.9.cloned.1.call-update) | async-done | bytes 983056 | tf_op jit(solution)/shard_map/psum | solution.py:55
  181.0 2.6 gather_fusion.9
  191.6 3.8 %fusion.105 = (bf16[4,24,2048]{2,0,1:T(4,128)(2,1)}, f32[4,24,2048]{2,0,1:T(4,128)}) fusion(f32[4,24,2048]{2,0,1:T(4,128)S(1)} %get-tuple-element.25, f32[4,24,2048]{2,1,0:T(8,128)} %reshape.104, f32[4,6,2048]{2,0,1:T(4,128)} %slice.198, f32[4,6,2048]{2,0,1:T(4,128)} %copy_select_fusion.2, f32[4,6,2048]{2,0,1:T(4,128)S(1)} %copy_select_fusion.3, ...), kind=kLoop, calls=%fused_computation.214 | loop fusion | flops 2949120 | bytes 4718592 | tf_op jit(solution)/shard_map/convert_element_type | solution.py:68
  199.1 3.4 %collective-permute-start.6 = (bf16[4,24,1,512]{3,1,2,0:T(8,128)(2,1)S(1)}, bf16[4,24,1,512]{3,1,2,0:T(8,128)(2,1)S(1)}, u32[]{:S(2)}, u32[]{:S(2)}) collective-permute-start(bf16[4,24,1,512]{3,1,2,0:T(8,128)(2,1)S(1)} %copy.235), channel_id=1, source_target_pairs={{0,4},{4,8},{8,12},{12,16},{16,20},{20,24},{24,28},{1,5},{5,9},{9,... | collective-permute-start | bytes 294920 | tf_op jit(solution)/shard_map/ppermute | solution.py:21
  206.3 2.8 collective-permute-done.7
  209.7 2.5 gather_fusion.13
  214.6 2.5 gather_fusion.15
  235.8 3.0 fusion.4
  243.6 11.8 %psum.69 = f32[6,2048]{1,0:T(8,128)S(1)} all-reduce(f32[6,2048]{1,0:T(8,128)S(1)} %bitcast.124), channel_id=1, replica_groups=mesh['space'=8,'scen'=4] {'scen'}, use_global_device_ids=true, to_apply=%region_9.13 | all-reduce | flops 12288 | bytes 98304 | tf_op jit(solution)/shard_map/psum | solution.py:55
  256.7 23.5 %all-reduce.7.cloned.1.call-done = (f32[16,6,2048]{2,0,1:T(8,128)}, f32[4,6,2048]{2,0,1:T(4,128)}) async-done(((f32[16,6,2048]{2,0,1:T(8,128)}, f32[4,6,2048]{2,0,1:T(4,128)}), (f32[16,6,2048]{2,0,1:T(8,128)}, f32[4,6,2048]{2,0,1:T(4,128)})) %all-reduce.7.cloned.1.call-update) | async-done | bytes 983056 | tf_op jit(solution)/shard_map/psum | solution.py:55
  283.0 2.7 gather_fusion.17
  (249 shorter events, 154.1 us)
Async XLA Ops:
  7.2 8.9 %copy-start.38 = (s32[2,16]{1,0:T(2,128)S(1)}, s32[2,16]{1,0:T(2,128)}, u32[]{:S(2)}) copy-start(s32[2,16]{1,0:T(2,128)} %param.18) | copy-start | bytes 388
  7.2 50.3 %all-reduce.11.cloned.1.call-start = ((), (), s32[]{:S(2)}) async-start(), calls=%async_computation.2 | async-start | bytes 1966080 | tf_op jit(solution)/shard_map/psum | solution.py:55
  8.3 28.1 %collective-permute-start = (bf16[4,24,1,512]{3,1,2,0:T(8,128)(2,1)S(1)}, bf16[4,24,1,512]{3,1,2,0:T(8,128)(2,1)S(1)}, u32[]{:S(2)}, u32[]{:S(2)}) collective-permute-start(bf16[4,24,1,512]{3,1,2,0:T(8,128)(2,1)S(1)} %get-tuple-element.41), channel_id=1, source_target_pairs={{0,4},{4,8},{8,12},{12,16},{16,20},{20,24},{24,28},{1,5},{5,9},{9,... | collective-permute-start | bytes 294920 | tf_op jit(solution)/shard_map/ppermute | solution.py:21
  13.2 23.3 %collective-permute-start.1 = (bf16[4,24,1,512]{3,1,2,0:T(8,128)(2,1)S(1)}, bf16[4,24,1,512]{3,1,2,0:T(8,128)(2,1)S(1)}, u32[]{:S(2)}, u32[]{:S(2)}) collective-permute-start(bf16[4,24,1,512]{3,1,2,0:T(8,128)(2,1)S(1)} %get-tuple-element.40), channel_id=1, source_target_pairs={{4,0},{8,4},{12,8},{16,12},{20,16},{24,20},{28,24},{5,1},{9,5},{13... | collective-permute-start | bytes 294920 | tf_op jit(solution)/shard_map/ppermute | solution.py:22
  16.2 18.4 %copy-start.26 = (s32[4]{0:T(128)}, s32[4]{0:T(128)S(1)}, u32[]{:S(2)}) copy-start(s32[4]{0:T(128)S(1)} %get-tuple-element.46) | copy-start | bytes 52
  16.2 18.4 %copy-start.28 = (s32[4]{0:T(128)}, s32[4]{0:T(128)S(1)}, u32[]{:S(2)}) copy-start(s32[4]{0:T(128)S(1)} %get-tuple-element.47) | copy-start | bytes 52
  18.7 159.5 %all-reduce.9.cloned.1.call-start = ((), (), s32[]{:S(2)}) async-start(), calls=%async_computation.1 | async-start | bytes 1966080 | tf_op jit(solution)/shard_map/psum | solution.py:55
  19.6 18.6 %copy-start.33 = (pred[4]{0:T(512)(128)(4,1)}, pred[4]{0:T(512)(128)(4,1)S(1)}, u32[]{:S(2)}) copy-start(pred[4]{0:T(512)(128)(4,1)S(1)} %compare_and_fusion.2) | copy-start | bytes 16
  19.8 37.8 %copy-start.36 = (f32[16]{0:T(128)}, f32[16]{0:T(128)S(1)}, u32[]{:S(2)}) copy-start(f32[16]{0:T(128)S(1)} %select_reduce_fusion) | copy-start | bytes 196
  20.4 17.2 %copy-start.24 = (s32[1024]{0:T(1024)}, s32[1024]{0:T(1024)S(1)}, u32[]{:S(2)}) copy-start(s32[1024]{0:T(1024)S(1)} %pad_clamp_fusion.2) | copy-start | bytes 12292
  60.3 9.2 %copy-start.1 = (f32[4,24,2048]{2,1,0:T(8,128)S(1)}, f32[4,24,2048]{2,1,0:T(8,128)}, u32[]{:S(2)}) copy-start(f32[4,24,2048]{2,1,0:T(8,128)} %param.15) | copy-start | bytes 2359300
  60.3 9.2 %copy-start.5 = (bf16[4,24,2048]{2,1,0:T(8,128)(2,1)S(1)}, bf16[4,24,2048]{2,1,0:T(8,128)(2,1)}, u32[]{:S(2)}) copy-start(bf16[4,24,2048]{2,1,0:T(8,128)(2,1)} %param.14) | copy-start | bytes 1179652
  60.3 9.2 %copy-start.14 = (f32[4,6,2048]{2,0,1:T(4,128)S(1)}, f32[4,6,2048]{2,0,1:T(4,128)}, u32[]{:S(2)}) copy-start(f32[4,6,2048]{2,0,1:T(4,128)} %slice.190) | copy-start | bytes 589828
  75.0 5.6 %collective-permute-start.2 = (bf16[4,24,1,512]{3,1,2,0:T(8,128)(2,1)S(1)}, bf16[4,24,1,512]{3,1,2,0:T(8,128)(2,1)S(1)}, u32[]{:S(2)}, u32[]{:S(2)}) collective-permute-start(bf16[4,24,1,512]{3,1,2,0:T(8,128)(2,1)S(1)} %copy.231), channel_id=1, source_target_pairs={{0,4},{4,8},{8,12},{12,16},{16,20},{20,24},{24,28},{1,5},{5,9},{9,... | collective-permute-start | bytes 294920 | tf_op jit(solution)/shard_map/ppermute | solution.py:21
  78.5 6.5 %collective-permute-start.3 = (bf16[4,24,1,512]{3,1,2,0:T(8,128)(2,1)S(1)}, bf16[4,24,1,512]{3,1,2,0:T(8,128)(2,1)S(1)}, u32[]{:S(2)}, u32[]{:S(2)}) collective-permute-start(bf16[4,24,1,512]{3,1,2,0:T(8,128)(2,1)S(1)} %copy.232), channel_id=1, source_target_pairs={{4,0},{8,4},{12,8},{16,12},{20,16},{24,20},{28,24},{5,1},{9,5},{13... | collective-permute-start | bytes 294920 | tf_op jit(solution)/shard_map/ppermute | solution.py:22
  116.3 25.8 %collective-permute-start.4 = (bf16[4,24,1,512]{3,1,2,0:T(8,128)(2,1)}, bf16[4,24,1,512]{3,1,2,0:T(8,128)(2,1)}, u32[]{:S(2)}, u32[]{:S(2)}) collective-permute-start(bf16[4,24,1,512]{3,1,2,0:T(8,128)(2,1)} %copy.233), channel_id=1, source_target_pairs={{0,4},{4,8},{8,12},{12,16},{16,20},{20,24},{24,28},{1,5},{5,9},{9,... | collective-permute-start | bytes 294920 | tf_op jit(solution)/shard_map/ppermute | solution.py:21
  140.5 6.9 %collective-permute-start.5 = (bf16[4,24,1,512]{3,1,2,0:T(8,128)(2,1)}, bf16[4,24,1,512]{3,1,2,0:T(8,128)(2,1)}, u32[]{:S(2)}, u32[]{:S(2)}) collective-permute-start(bf16[4,24,1,512]{3,1,2,0:T(8,128)(2,1)} %copy.234), channel_id=1, source_target_pairs={{4,0},{8,4},{12,8},{16,12},{20,16},{24,20},{28,24},{5,1},{9,5},{13... | collective-permute-start | bytes 294920 | tf_op jit(solution)/shard_map/ppermute | solution.py:22
  141.8 138.4 %all-reduce.7.cloned.1.call-start = ((), (), s32[]{:S(2)}) async-start(), calls=%async_computation | async-start | bytes 1966080 | tf_op jit(solution)/shard_map/psum | solution.py:55
  199.1 5.6 %collective-permute-start.6 = (bf16[4,24,1,512]{3,1,2,0:T(8,128)(2,1)S(1)}, bf16[4,24,1,512]{3,1,2,0:T(8,128)(2,1)S(1)}, u32[]{:S(2)}, u32[]{:S(2)}) collective-permute-start(bf16[4,24,1,512]{3,1,2,0:T(8,128)(2,1)S(1)} %copy.235), channel_id=1, source_target_pairs={{0,4},{4,8},{8,12},{12,16},{16,20},{20,24},{24,28},{1,5},{5,9},{9,... | collective-permute-start | bytes 294920 | tf_op jit(solution)/shard_map/ppermute | solution.py:21
  202.6 6.5 %collective-permute-start.7 = (bf16[4,24,1,512]{3,1,2,0:T(8,128)(2,1)S(1)}, bf16[4,24,1,512]{3,1,2,0:T(8,128)(2,1)S(1)}, u32[]{:S(2)}, u32[]{:S(2)}) collective-permute-start(bf16[4,24,1,512]{3,1,2,0:T(8,128)(2,1)S(1)} %copy.236), channel_id=1, source_target_pairs={{4,0},{8,4},{12,8},{16,12},{20,16},{24,20},{28,24},{5,1},{9,5},{13... | collective-permute-start | bytes 294920 | tf_op jit(solution)/shard_map/ppermute | solution.py:22
  242.2 38.0 %copy-start.37 = (f32[16]{0:T(128)S(1)}, f32[16]{0:T(128)}, u32[]{:S(2)}) copy-start(f32[16]{0:T(128)} %copy-done.36) | copy-start | bytes 196
  283.0 10.0 %copy-start.3 = (f32[4,24,2048]{2,0,1:T(4,128)S(1)}, f32[4,24,2048]{2,0,1:T(4,128)}, u32[]{:S(2)}) copy-start(f32[4,24,2048]{2,0,1:T(4,128)} %copy-done.2) | copy-start | bytes 2359300
  283.0 10.0 %slice-start = ((f32[4,24,2048]{2,0,1:T(4,128)}), f32[4,6,2048]{2,0,1:T(4,128)S(1)}, s32[]{:S(2)}) async-start(f32[4,24,2048]{2,0,1:T(4,128)} %copy-done.2), calls=%async_computation.3 | async-start | bytes 393216 | tf_op jit(solution)/shard_map/slice | solution.py:34
  283.0 10.0 %copy-start.13 = (f32[4,6,2048]{2,0,1:T(4,128)S(1)}, f32[4,6,2048]{2,0,1:T(4,128)}, u32[]{:S(2)}) copy-start(f32[4,6,2048]{2,0,1:T(4,128)} %copy-done.11) | copy-start | bytes 589828
  (29 other events, 116.3 us)
Sparse Core Ops, SparseCore 0:
  18.8 38.6 all-reduce.10
  141.9 36.2 all-reduce.8
  243.8 36.3 all-reduce.6
where the time goes:
time: 305 us; the launch traced here: 302 us
  local copies, waits for them, and re-layouts  107 us (35%)
  waiting for transfers between devices  48.7 us (16%)
  other arithmetic  45.4 us (15%)
  blocking collectives  35.9 us (12%)
  matrix products  27.5 us (9%)
  starting transfers between devices  22.5 us (7%)
  between operations  14.6 us (5%)
    psum x3, waiting for transfers between devices, tree_center(): lax.psum((root_term, first_term, second_term), 'scen')  40.1 us
    psum x3, blocking collectives, tree_center(): lax.psum((root_term, first_term, second_term), 'scen')  35.9 us
    gather x12, local copies, waits for them, and re-layouts, descend(): jnp.take(extended, local_cone[:, cone_slot], axis=2).reshape(-1, TILE)  23.2 us
    dot_general x12, matrix products, descend(): jnp.dot(picked, patterns[cone_slot], preferred_element_type=jnp.float32)  16.7 us
    ppermute x4, starting transfers between devices, extended_2(): before = lax.ppermute(last, axis, up)  16.6 us
    reshape x12, local copies, waits for them, and re-layouts, descend(): jnp.take(extended, local_cone[:, cone_slot], axis=2).reshape(-1, TILE)  13.9 us
    unnamed x98, local copies, waits for them, and re-layouts  12.5 us
    convert_element_type x3, other arithmetic, descend(): rounded = fraction.astype(jnp.bfloat16)  11.6 us
  transfers between devices with their start and end apart: 11, of which 8 were waited for; matrix products, arithmetic and copies ran while one was open for 20% of the time, Pallas kernels for 0%

commit v1 on v0

v1 whole, which is shorter than its diff:
```python
import functools
import jax
import jax.numpy as jnp
from jax import lax
from jax.experimental import pallas as pl
from jax.experimental.pallas import tpu as pltpu
from jax.sharding import PartitionSpec as P

TILE = 512
SECTIONS = 4
NODES1 = 4
NODES2 = 16
ITERS = 2
PG_STEPS = 2
SUB = 8
AXES = ("space", "scen")
CHAINS = ((0, 16), (16, 24))

f32, bf16 = jnp.float32, jnp.bfloat16
VMEM = pl.BlockSpec(memory_space=pltpu.VMEM)
SMEM = pl.BlockSpec(memory_space=pltpu.SMEM)
CORE, EDGE, INNER, SLOT_IN, SLOT_OUT, END, SLOT_EDGE, SLOT_OTHER, NODES = range(9)


def call(kernel, name, control, arrays, out):
    shapes = [jax.ShapeDtypeStruct(s, d) for s, d in out]
    return pl.pallas_call(
        kernel,
        out_shape=shapes,
        in_specs=[SMEM] * len(control) + [VMEM] * len(arrays),
        out_specs=[VMEM] * len(shapes),
        name=name,
        compiler_params=pltpu.CompilerParams(vmem_limit_bytes=48 << 20),
    )(*control, *arrays)


def lanes(tile):
    return pl.ds(pl.multiple_of(tile * TILE, TILE), TILE)


class Plan:
    def __init__(self, mesh, fraction, cone_list, node_list):
        self.spaces, self.scens = mesh.shape["space"], mesh.shape["scen"]
        self.rank, self.periods, width = fraction.shape
        self.tiles = cone_list.shape[0]
        self.quarter = self.periods // SECTIONS
        self.local = 2 * self.rank
        self.second = node_list.shape[1] > NODES2
        self.blocks = 1 + NODES1 + (NODES2 if self.second else 0)
        self.reach = (3 if self.second else 2) * self.quarter
        self.chains = tuple((lo, hi) for lo, hi in CHAINS)

    def averaged(self, chain):
        return chain[0] < self.reach

    def section(self, low, which):
        first, last = which * self.quarter, (which + 1) * self.quarter
        if low + SUB <= first or low >= last:
            return None
        if first <= low and low + SUB <= last:
            return True
        period = low + lax.broadcasted_iota(jnp.int32, (SUB, TILE), 0)
        return (period >= first) & (period < last)


def put(mask, new, old):
    return old if mask is None else new if mask is True else jnp.where(mask, new, old)


def partial_means(plan, chain, control, weights, edge, inner, sums):
    lo, hi = chain
    size = hi - lo
    for side, source in enumerate((edge, inner)):
        for block in range(plan.blocks):
            which = 0 if block == 0 else 1 if block <= NODES1 else 2
            total = jnp.zeros((SUB, TILE), f32)
            for low in range(lo, hi, SUB):
                mask = plan.section(low, which)
                if mask is None:
                    continue
                part = jnp.zeros((SUB, TILE), f32)
                for j in range(plan.local):
                    weight = weights[which * plan.local + j]
                    if which:
                        node = control[NODES + (which - 1) * plan.local + j]
                        first = 1 if which == 1 else 1 + NODES1
                        weight = jnp.where(node == block - first, weight, 0.0)
                    row = j * size + low - lo
                    part = part + weight * source[row : row + SUB, :]
                total = total + put(mask, part, jnp.zeros_like(part))
            sums[block, :, side * TILE : (side + 1) * TILE] = total


def center_rows(plan, low, side, nodes, means, value):
    span = slice(side * TILE, (side + 1) * TILE)
    value = put(plan.section(low, 0), means(0, span), value) if plan.section(low, 0) is not None else value
    mask = plan.section(low, 1)
    if mask is not None:
        value = put(mask, means(1 + nodes(0), span), value)
    mask = plan.section(low, 2)
    if plan.second and mask is not None:
        value = put(mask, means(1 + NODES1 + nodes(1), span), value)
    return value


def send_fraction(plan, control, start, out):
    other = 1 - control[CORE]
    edge, inner = other * (plan.tiles - 1), 1 + other * (plan.tiles - 3)
    out[0] = start[:, :, lanes(edge)]
    out[1] = start[:, :, lanes(inner)]


def send_drive(plan, control, ore, dual, out):
    other = 1 - control[CORE]
    for k, tile in enumerate((other * (plan.tiles - 1), 1 + other * (plan.tiles - 3))):
        out[k] = ore[:, :, lanes(tile)].astype(f32) - dual[:, :, lanes(tile)]


def assemble(plan, control, own, came, out):
    core = control[CORE]
    for (lo, hi), pair in zip(plan.chains, out):
        size = hi - lo
        for k, ref in enumerate(pair):
            for r in range(plan.rank):
                mine = pl.multiple_of((core * plan.rank + r) * size, SUB)
                theirs = pl.multiple_of(((1 - core) * plan.rank + r) * size, SUB)
                ref[pl.ds(mine, size), :] = own(k, r, lo, hi).astype(f32)
                ref[pl.ds(theirs, size), :] = came[k, r, lo:hi, :].astype(f32)


def start_kernel(plan, control, weights, start, came, *outs):
    n = len(plan.chains)
    state = [outs[2 * c : 2 * c + 2] for c in range(n)]
    sends = [outs[2 * n + 2 * c : 2 * n + 2 * c + 2] for c in range(n)]
    tiles = (control[EDGE], control[INNER])
    assemble(plan, control, lambda k, r, lo, hi: start[r, lo:hi, lanes(tiles[k])], came, state)
    for pair, send in zip(state, sends):
        for ref, out in zip(pair, send):
            out[...] = ref[...].astype(bf16)
    at = 4 * n
    for c, chain in enumerate(plan.chains):
        if plan.averaged(chain):
            partial_means(plan, chain, control, weights, *state[c], outs[at])
            at += 1


def drive_kernel(plan, control, ore, dual, came, *outs):
    tiles = (control[EDGE], control[INNER])

    def own(k, r, lo, hi):
        return ore[r, lo:hi, lanes(tiles[k])].astype(f32) - dual[r, lo:hi, lanes(tiles[k])]

    assemble(plan, control, own, came, [outs[2 * c : 2 * c + 2] for c in range(len(plan.chains))])


def inside(plan, chain, first, last_round, final, control, edge, inner, halo, drive_e, drive_n, patterns, *rest):
    lo, hi = chain
    size = hi - lo
    averaged = plan.averaged(chain)
    rest = list(rest)
    pull_e, pull_n = drive_e, drive_n
    if first:
        means_refs = (rest.pop(0), rest.pop(0)) if averaged else None
    base_e, next_n, send_n = rest[:3]
    rest = rest[3:]
    if first:
        pull_e, pull_n = rest[:2]
        rest = rest[2:]
        moved = rest[:2] if last_round and averaged else None
        if averaged:
            means = lambda block, span: means_refs[0][block, :, span] + means_refs[1][block, :, span]
        for side, (value, drive, pull) in enumerate(((edge, drive_e, pull_e), (inner, drive_n, pull_n))):
            for j in range(plan.local):
                for low in range(lo, hi, SUB):
                    rows = slice(j * size + low - lo, j * size + low - lo + SUB)
                    now = value[rows, :]
                    mean = now
                    if averaged:
                        nodes = lambda which: control[NODES + which * plan.local + j]
                        mean = center_rows(plan, low, side, nodes, means, now)
                    if last_round:
                        gap = now - mean
                        if averaged:
                            moved[side][rows, :] = gap
                        pull[rows, :] = drive[rows, :] - gap + mean
                    else:
                        pull[rows, :] = drive[rows, :] + mean
    round_e, round_n = edge[...].astype(bf16), inner[...].astype(bf16)
    dot = functools.partial(jnp.dot, preferred_element_type=f32)
    cone = dot(round_e, patterns[0]) + dot(round_n, patterns[control[SLOT_IN]])
    value = edge[...]
    base_e[...] = value - 0.4 * ((value - cone) + value - pull_e[...])
    cone = dot(round_n, patterns[0]) + dot(round_e, patterns[control[SLOT_EDGE]]) + dot(halo[...], patterns[control[SLOT_OTHER]])
    value = inner[...]
    value = jnp.clip(value - 0.4 * ((value - cone) + value - pull_n[...]), 0.0, 1.0)
    next_n[...] = value
    send_n[...] = value.astype(bf16)
    if final:
        count = plan.rank * size
        rest[0][...] = next_n[pl.ds(pl.multiple_of((1 - control[CORE]) * count, SUB), count), :]


def outside(plan, chain, means, final, control, weights, base, halo, round_e, patterns, *rest):
    rest = list(rest)
    inner = rest.pop(0) if means else None
    next_e, send_e = rest[:2]
    lhs = jnp.where(control[END] == 1, round_e[...].astype(f32), halo[...].astype(f32)).astype(bf16)
    cone = jnp.dot(lhs, patterns[control[SLOT_OUT]], preferred_element_type=f32)
    value = jnp.clip(base[...] + 0.4 * cone, 0.0, 1.0)
    next_e[...] = value
    send_e[...] = value.astype(bf16)
    rest = rest[2:]
    if means:
        partial_means(plan, chain, control, weights, next_e, inner, rest.pop(0))
    if final:
        count = plan.rank * (chain[1] - chain[0])
        rest[0][...] = next_e[pl.ds(pl.multiple_of((1 - control[CORE]) * count, SUB), count), :]


def finish_kernel(plan, control, *refs):
    refs = list(refs)
    dual = refs.pop(0)
    mean_refs = [(refs.pop(0), refs.pop(0)), (refs.pop(0), refs.pop(0))]
    fraction, dual_out = refs[-2:]
    core = control[CORE]
    tiles = ((control[EDGE], control[INNER]), ((1 - core) * (plan.tiles - 1), 1 + (1 - core) * (plan.tiles - 3)))
    at = 0
    for chain in plan.chains:
        lo, hi = chain
        size = hi - lo
        held = refs[at : at + 2]
        came = refs[at + 2 : at + 4]
        at += 4
        averaged = plan.averaged(chain)
        if averaged:
            moved, moved_came = refs[at : at + 2], refs[at + 2 : at + 4]
            at += 4
        for part in range(2):
            pair = mean_refs[part]
            means = lambda block, span: pair[0][block, :, span] + pair[1][block, :, span]
            for side in range(2):
                where = lanes(tiles[part][side])
                for r in range(plan.rank):
                    for low in range(lo, hi, SUB):
                        if part == 0:
                            row = pl.multiple_of((core * plan.rank + r) * size + low - lo, SUB)
                            now = held[side][pl.ds(row, SUB), :]
                        else:
                            row = r * size + low - lo
                            now = came[side][row : row + SUB, :]
                        out = (r, slice(low, low + SUB), where)
                        fraction[out] = now
                        price = dual[out]
                        if averaged and low < plan.reach:
                            nodes = lambda which: control[NODES + which * plan.local + core * plan.rank + r]
                            mean = center_rows(plan, low, side, nodes, means, now)
                            gap = moved[side][pl.ds(row, SUB), :] if part == 0 else moved_came[side][row : row + SUB, :]
                            price = (price + gap) + (now - mean)
                        dual_out[out] = price


def partners(plan):
    pairs = []
    for i in range(plan.spaces):
        for s in range(plan.scens):
            to = i + 1 if s % 2 else i - 1
            if 0 <= to < plan.spaces:
                pairs.append((i * plan.scens + s, to * plan.scens + (s ^ 1)))
            else:
                pairs.append((i * plan.scens + s, i * plan.scens + (s ^ 2 if plan.scens % 4 == 0 else s)))
    return pairs


def control_of(plan, cone_list, node_list, probability):
    core = lax.axis_index("scen") % 2
    edge = core * (plan.tiles - 1)
    inner = 1 + core * (plan.tiles - 3)
    local = cone_list - lax.axis_index("space") * plan.tiles
    row_e = lax.dynamic_index_in_dim(local, edge, 0, keepdims=False)
    row_n = lax.dynamic_index_in_dim(local, inner, 0, keepdims=False)
    slot_in = jnp.where(row_e[1] == inner, 1, 2)
    slot_out = 3 - slot_in
    end = (jnp.where(slot_out == 1, row_e[1], row_e[2]) == edge).astype(jnp.int32)
    slot_edge = jnp.where(row_n[1] == edge, 1, 2)
    base = (lax.axis_index("scen") // 2) * plan.local
    nodes = lax.dynamic_slice_in_dim(node_list, base, plan.local, 1).reshape(-1)
    head = jnp.stack([core, edge, inner, slot_in, slot_out, end, slot_edge, 3 - slot_edge]).astype(jnp.int32)
    rows = [probability / jnp.sum(probability)]
    for row in range(2):
        same = node_list[row][:, None] == node_list[row][None, :]
        rows.append(probability / jnp.sum(jnp.where(same, probability[None, :], 0.0), axis=1))
    weights = lax.dynamic_slice_in_dim(jnp.stack(rows), base, plan.local, 1).reshape(-1)
    return jnp.concatenate([head, nodes]), weights


def tiled(plan, start, ore, dual, patterns, cone_list, node_list, probability):
    core = (lax.axis_index("scen") % 2).astype(jnp.int32)
    place = jnp.stack([core, core * (plan.tiles - 1), 1 + core * (plan.tiles - 3)])
    control, weights = control_of(plan, cone_list, node_list, probability)
    flip = [(i, i ^ 1) for i in range(plan.scens)]
    edges = partners(plan)
    swap = lambda x: lax.ppermute(x, "scen", flip)
    outer = lambda x: lax.ppermute(x, AXES, edges)
    half = (2, plan.rank, plan.periods, TILE)
    sums = (plan.blocks, SUB, 2 * TILE)
    chains = plan.chains
    rows = [plan.local * (hi - lo) for lo, hi in chains]
    part = lambda f, *a: functools.partial(f, plan, *a)

    def across(x, stop):
        bits = [1 << b for b in range(1, plan.scens.bit_length() - 1)]
        other = None
        for n, bit in enumerate(bits):
            if n:
                x = x + other
            other = lax.ppermute(x, "scen", [(i, i ^ bit) for i in range(plan.scens)])
        return x, (jnp.zeros_like(x) if other is None else other)

    came = swap(call(part(send_fraction), "send_fraction", [place], [start], [(half, bf16)])[0])
    drive_came = swap(call(part(send_drive), "send_drive", [place], [ore, dual], [(half, f32)])[0])
    n_avg = sum(plan.averaged(c) for c in chains)
    got = call(
        part(start_kernel), "start", [control, weights], [start, came],
        [((r, TILE), f32) for r in rows for _ in range(2)] + [((r, TILE), bf16) for r in rows for _ in range(2)] + [(sums, f32)] * n_avg,
    )
    n = len(chains)
    state = [list(got[2 * c : 2 * c + 2]) for c in range(n)]
    rounded = [list(got[2 * n + 2 * c : 2 * n + 2 * c + 2]) for c in range(n)]
    halo = [[outer(rounded[c][0]), swap(rounded[c][1])] for c in range(n)]
    means = across(sum(got[4 * n + 1 :], got[4 * n]), 0)
    got = call(part(drive_kernel), "drive", [control], [ore, dual, drive_came], [((r, TILE), f32) for r in rows for _ in range(2)])
    drive = [list(got[2 * c : 2 * c + 2]) for c in range(n)]
    moved, pull = [None] * n, [None] * n
    sent = [[None, None] for _ in range(n)]
    for step in range(ITERS * PG_STEPS):
        first = step % PG_STEPS == 0
        closing = step % PG_STEPS == PG_STEPS - 1
        final = step == ITERS * PG_STEPS - 1
        last_round = step >= PG_STEPS
        sums_now = []
        for c, chain in enumerate(chains):
            averaged = plan.averaged(chain)
            shape = (rows[c], TILE)
            quart = (plan.rank * (chain[1] - chain[0]), TILE)
            arrays = [*state[c], halo[c][1], *(drive if first else pull)[c], patterns]
            outs = [(shape, f32), (shape, f32), (shape, bf16)]
            if first:
                arrays += list(means) if averaged else []
                outs += [(shape, f32)] * 2
                outs += [(shape, f32)] * 2 if last_round and averaged else []
            outs += [(quart, f32)] if final else []
            got = call(part(inside, chain, first, last_round, final), f"inside_{step}_{c}", [control], arrays, outs)
            base, state[c][1], rounded_n = got[:3]
            if first:
                pull[c] = list(got[3:5])
                if last_round and averaged:
                    moved[c] = list(got[5:7])
            if final:
                sent[c][1] = swap(got[-1])
            else:
                halo_n = swap(rounded_n)
            with_means = closing and averaged
            arrays = [base, halo[c][0], rounded[c][0], patterns] + ([state[c][1]] if with_means else [])
            outs = [(shape, f32), (shape, bf16)] + ([(sums, f32)] if with_means else []) + ([(quart, f32)] if final else [])
            got = call(part(outside, chain, with_means, final), f"outside_{step}_{c}", [control, weights], arrays, outs)
            state[c][0], rounded[c][0] = got[:2]
            if with_means:
                sums_now.append(got[2])
            if final:
                sent[c][0] = swap(got[-1])
            else:
                halo[c] = [outer(rounded[c][0]), halo_n]
        if closing:
            means = across(sum(sums_now[1:], sums_now[0]), 0)
    count = lambda c: plan.rank * (chains[c][1] - chains[c][0])
    theirs = (swap(means[0]), swap(means[1]))
    arrays = [dual, *means, *theirs]
    for c in range(n):
        arrays += state[c] + sent[c]
        if plan.averaged(chains[c]):
            rest = [lax.dynamic_slice_in_dim(m, (1 - core) * count(c), count(c), 0) for m in moved[c]]
            arrays += moved[c] + [swap(m) for m in rest]
    whole = start.shape
    return tuple(call(part(finish_kernel), "finish", [control], arrays, [(whole, f32), (whole, f32)]))


def solution(mesh):
    def body(start, ore, dual, patterns, cone_list, node_list, probability):
        plan = Plan(mesh, start, cone_list, node_list)
        assert plan.tiles == 4 and plan.scens % 2 == 0 and plan.periods % SUB == 0
        return tiled(plan, start, ore, dual, patterns, cone_list, node_list, probability)

    split = P("scen", None, "space")
    in_specs = (split, split, split, P(), P("space", None), P(), P())
    return jax.shard_map(body, mesh=mesh, in_specs=in_specs, out_specs=(split, split), check_vma=False)
```

time: 305 us -> 67.4 us (0.22)
  local copies, waits for them, and re-layouts: 107 us -> 6.69 us
  other arithmetic: 45.4 us -> 1.62 us
  waiting for transfers between devices: 48.7 us -> 8.72 us
  blocking collectives: 35.9 us -> 0 us
  matrix products: 27.5 us -> 0 us
  Pallas kernels: 0 us -> 24.7 us
  between operations: 14.6 us -> 3.38 us
    psum x3 -> x0, waiting for transfers between devices: 40.1 us -> none  [tree_center(): lax.psum((root_term, first_term, second_term), 'scen')]
    gather x18 -> x0, local copies, waits for them, and re-layouts: 38.2 us -> none  [the longest x12 23.2 us: descend(): jnp.take(extended, local_cone[:, cone_slot], axis=2).reshape(-1, TILE)]
    psum x3 -> x0, blocking collectives: 35.9 us -> none  [tree_center(): lax.psum((root_term, first_term, second_term), 'scen')]
    reshape x20 -> x2, local copies, waits for them, and re-layouts: 28.6 us -> 0.16 us  [the longest x1 0.08 us: control_of(): lax.dynamic_slice_in_dim(jnp.stack(rows), base, plan.local, 1).reshape(-1)]
    dot_general x21 -> x0, matrix products: 27.5 us -> none  [the longest x12 16.7 us: descend(): jnp.dot(picked, patterns[cone_slot], preferred_element_type=jnp.float32)]
    pallas_call x0 -> x21, Pallas kernels: none -> 24.7 us  [call(): pl.pallas_call(kernel, out_shape=shapes, in_specs=[SMEM] * len(control) +...]
    select_n x20 -> x0, other arithmetic: 15.2 us -> none  [the longest x14 7.88 us: descend(): jnp.take(extended, local_cone[:, cone_slot], axis=2).reshape(-1, TILE)]
    convert_element_type x3 -> x0, other arithmetic: 11.6 us -> none  [descend(): rounded = fraction.astype(jnp.bfloat16)]
  transfers between devices with their start and end apart: 11 -> 29, of which waited for: 8 -> 10; matrix products, arithmetic and copies ran while one was open for 20% -> 5% of each run, Pallas kernels for 0% -> 31%
where the time goes in v1:
time: 67.4 us; the launch traced here: 66.9 us
  Pallas kernels  24.7 us (37%)
  starting transfers between devices  21.8 us (32%)
  waiting for transfers between devices  8.72 us (13%)
  local copies, waits for them, and re-layouts  6.69 us (10%)
  between operations  3.38 us (5%)
  other arithmetic  1.62 us (2%)
    pallas_call x21, Pallas kernels, call(): pl.pallas_call(kernel, out_shape=shapes, in_specs=[SMEM] * len(control) +...  24.7 us
    ppermute x8, starting transfers between devices, tiled(): outer = lambda x: lax.ppermute(x, AXES, edges)  8.34 us
    ppermute x18, starting transfers between devices, tiled(): swap = lambda x: lax.ppermute(x, 'scen', flip)  8.2 us
    ppermute x3, starting transfers between devices, across(): other = lax.ppermute(x, 'scen', [(i, i ^ bit) for i in range(plan.scens)])  5.26 us
    unnamed x30, local copies, waits for them, and re-layouts  4.95 us
    ppermute x3, waiting for transfers between devices, across(): other = lax.ppermute(x, 'scen', [(i, i ^ bit) for i in range(plan.scens)])  4.38 us
    ppermute x8, waiting for transfers between devices, tiled(): outer = lambda x: lax.ppermute(x, AXES, edges)  2.89 us
    ppermute x18, waiting for transfers between devices, tiled(): swap = lambda x: lax.ppermute(x, 'scen', flip)  1.44 us
  transfers between devices with their start and end apart: 29, of which 10 were waited for; matrix products, arithmetic and copies ran while one was open for 5% of the time, Pallas kernels for 31%

profile of v1, /device:TPU:0, one launch (start us, length us, event | category | flops | bytes accessed | tf_op | source)
XLA Modules:
  0.0 66.9 jit_solution(521452115014519113)
XLA Ops:
  1.8 1.2 %send_fraction.1 = bf16[2,4,24,512]{3,2,1,0:T(8,128)(2,1)} custom-call(s32[3]{0:T(128)S(1)} %pad_add_fusion.control, bf16[4,24,2048]{2,1,0:T(8,128)(2,1)S(1)} %copy-done.4), custom_call_target="tpu_custom_call" | custom-call | tf_op jit(solution)/shard_map/send_fraction/pallas_call | solution.py:27
  13.0 2.9 %collective-permute-start.3 = (f32[5,8,1024]{2,1,0:T(8,128)S(1)}, f32[5,8,1024]{2,1,0:T(8,128)S(1)}, u32[]{:S(2)}, u32[]{:S(2)}) collective-permute-start(f32[5,8,1024]{2,1,0:T(8,128)S(1)} %get-tuple-element.72.rest_0_), channel_id=1, source_target_pairs={{0,2},{1,3},{2,0},{3,1},{4,6},{5,7},{6,4},{7,5},{8,10},{9,11},{10,... | collective-permute-start | bytes 491528 | tf_op jit(solution)/shard_map/ppermute | solution.py:316
  16.2 1.1 %copy-done.2 = f32[4,24,2048]{2,1,0:T(8,128)S(1)} copy-done((f32[4,24,2048]{2,1,0:T(8,128)S(1)}, f32[4,24,2048]{2,1,0:T(8,128)}, u32[]{:S(2)}) %copy-start.2) | copy-done | bytes 786456
  17.9 2.5 %collective-permute-done.3.rest_1_ = f32[5,8,1024]{2,1,0:T(8,128)S(1)} collective-permute-done((f32[5,8,1024]{2,1,0:T(8,128)S(1)}, f32[5,8,1024]{2,1,0:T(8,128)S(1)}, u32[]{:S(2)}, u32[]{:S(2)}) %collective-permute-start.3) | collective-permute-done | bytes 163872 | tf_op jit(solution)/shard_map/ppermute | solution.py:316
  20.4 1.2 %inside_0_0.1 = (f32[128,512]{1,0:T(8,128)S(1)}, f32[128,512]{1,0:T(8,128)S(1)}, bf16[128,512]{1,0:T(8,128)(2,1)S(1)}, f32[128,512]{1,0:T(8,128)S(1)}, f32[128,512]{1,0:T(8,128)S(1)}) custom-call(s32[24]{0:T(128)S(1)} %concatenate.3.control, f32[128,512]{1,0:T(8,128)S(1)} %get-tuple-element.67.edge, f32[128,512]{1,0:T(8,128)S(1)} %get-tuple-element.68.inner, ...), custom_call_target="tpu_custom_call" | custom-call | tf_op jit(solution)/shard_map/inside_0_0/pallas_call | solution.py:27
  22.6 1.8 %collective-permute-start.6 = (bf16[128,512]{1,0:T(8,128)(2,1)S(1)}, bf16[128,512]{1,0:T(8,128)(2,1)S(1)}, u32[]{:S(2)}, u32[]{:S(2)}) collective-permute-start(bf16[128,512]{1,0:T(8,128)(2,1)S(1)} %get-tuple-element.81.round_e), channel_id=1, source_target_pairs={{0,2},{1,4},{2,0},{3,6},{4,1},{5,8},{6,3},{7,10},{8,5},{9,12},{10,... | collective-permute-start | bytes 393224 | tf_op jit(solution)/shard_map/ppermute | solution.py:303
  25.6 2.1 %collective-permute-done.6.halo = bf16[128,512]{1,0:T(8,128)(2,1)S(1)} collective-permute-done((bf16[128,512]{1,0:T(8,128)(2,1)S(1)}, bf16[128,512]{1,0:T(8,128)(2,1)S(1)}, u32[]{:S(2)}, u32[]{:S(2)}) %collective-permute-start.6) | collective-permute-done | bytes 131104 | tf_op jit(solution)/shard_map/ppermute | solution.py:303
  28.6 1.8 %collective-permute-start.8 = (f32[5,8,1024]{2,1,0:T(8,128)S(1)}, f32[5,8,1024]{2,1,0:T(8,128)S(1)}, u32[]{:S(2)}, u32[]{:S(2)}) collective-permute-start(f32[5,8,1024]{2,1,0:T(8,128)S(1)} %get-tuple-element.85.rest_0_), channel_id=1, source_target_pairs={{0,2},{1,3},{2,0},{3,1},{4,6},{5,7},{6,4},{7,5},{8,10},{9,11},{10,... | collective-permute-start | bytes 491528 | tf_op jit(solution)/shard_map/ppermute | solution.py:316
  30.7 1.8 %collective-permute-start.19 = (bf16[64,512]{1,0:T(8,128)(2,1)S(1)}, bf16[64,512]{1,0:T(8,128)(2,1)S(1)}, u32[]{:S(2)}, u32[]{:S(2)}) collective-permute-start(bf16[64,512]{1,0:T(8,128)(2,1)S(1)} %get-tuple-element.104), channel_id=1, source_target_pairs={{0,1},{1,0},{2,3},{3,2},{4,5},{5,4},{6,7},{7,6},{8,9},{9,8},{10,11... | collective-permute-start | bytes 196616 | tf_op jit(solution)/shard_map/ppermute | solution.py:302
  33.0 1.9 %collective-permute-done.8.rest_1_ = f32[5,8,1024]{2,1,0:T(8,128)S(1)} collective-permute-done((f32[5,8,1024]{2,1,0:T(8,128)S(1)}, f32[5,8,1024]{2,1,0:T(8,128)S(1)}, u32[]{:S(2)}, u32[]{:S(2)}) %collective-permute-start.8) | collective-permute-done | bytes 163872 | tf_op jit(solution)/shard_map/ppermute | solution.py:316
  34.9 1.2 %inside_2_0.1 = (f32[128,512]{1,0:T(8,128)S(1)}, f32[128,512]{1,0:T(8,128)S(1)}, bf16[128,512]{1,0:T(8,128)(2,1)S(1)}, f32[128,512]{1,0:T(8,128)S(1)}, f32[128,5...) custom-call(s32[24]{0:T(128)S(1)} %concatenate.3.control, f32[128,512]{1,0:T(8,128)S(1)} %get-tuple-element.83.edge, ...), custom_call_target="tpu_custom_call" | custom-call | tf_op jit(solution)/shard_map/inside_2_0/pallas_call | solution.py:27
  37.1 1.8 %collective-permute-start.11 = (bf16[128,512]{1,0:T(8,128)(2,1)S(1)}, bf16[128,512]{1,0:T(8,128)(2,1)S(1)}, u32[]{:S(2)}, u32[]{:S(2)}) collective-permute-start(bf16[128,512]{1,0:T(8,128)(2,1)S(1)} %get-tuple-element.94.round_e), channel_id=1, source_target_pairs={{0,2},{1,4},{2,0},{3,6},{4,1},{5,8},{6,3},{7,10},{8,5},{9,12},{10,... | collective-permute-start | bytes 393224 | tf_op jit(solution)/shard_map/ppermute | solution.py:303
  38.9 1.2 %inside_0_1.1 = (f32[64,512]{1,0:T(8,128)S(1)}, f32[64,512]{1,0:T(8,128)S(1)}, bf16[64,512]{1,0:T(8,128)(2,1)S(1)}, f32[64,512]{1,0:T(8,128)S(1)}, f32[64,512]{1,0:T(8,128)S(1)}) custom-call(s32[24]{0:T(128)S(1)} %concatenate.3.control, f32[64,512]{1,0:T(8,128)S(1)} %get-tuple-element.102.edge, f32[64,512]{1,0:T(8,128)S(1)} %get-tuple-element.103.inner, ...), custom_call_target="tpu_custom_call" | custom-call | tf_op jit(solution)/shard_map/inside_0_1/pallas_call | solution.py:27
  41.2 1.6 %collective-permute-start.22 = (bf16[64,512]{1,0:T(8,128)(2,1)S(1)}, bf16[64,512]{1,0:T(8,128)(2,1)S(1)}, u32[]{:S(2)}, u32[]{:S(2)}) collective-permute-start(bf16[64,512]{1,0:T(8,128)(2,1)S(1)} %get-tuple-element.115.round_e), channel_id=1, source_target_pairs={{0,2},{1,4},{2,0},{3,6},{4,1},{5,8},{6,3},{7,10},{8,5},{9,12},{10,... | collective-permute-start | bytes 196616 | tf_op jit(solution)/shard_map/ppermute | solution.py:303
  42.7 1.8 %inside_1_1.1 = (f32[64,512]{1,0:T(8,128)S(1)}, f32[64,512]{1,0:T(8,128)S(1)}, bf16[64,512]{1,0:T(8,128)(2,1)}) custom-call(s32[24]{0:T(128)S(1)} %concatenate.3.control, f32[64,512]{1,0:T(8,128)S(1)} %get-tuple-element.109.edge, f32[64,512]{1,0:T(8,128)S(1)} %get-tuple-element.110.inner, bf16[64,512]{1,0:T(8,128)(2,1)S(1)} %collective-permute-done.21.halo, ...), custom_call_target="tpu_custom_call" | custom-call | tf_op jit(solution)/shard_map/inside_1_1/pallas_call | solution.py:27
  46.3 1.6 %collective-permute-start.24 = (bf16[64,512]{1,0:T(8,128)(2,1)S(1)}, bf16[64,512]{1,0:T(8,128)(2,1)}, u32[]{:S(2)}, u32[]{:S(2)}) collective-permute-start(bf16[64,512]{1,0:T(8,128)(2,1)S(1)} %get-tuple-element.120.round_e), channel_id=1, source_target_pairs={{0,2},{1,4},{2,0},{3,6},{4,1},{5,8},{6,3},{7,10},{8,5},{9,12},{10,... | collective-permute-start | bytes 196616 | tf_op jit(solution)/shard_map/ppermute | solution.py:303
  47.8 1.8 %inside_3_0.1 = (f32[128,512]{1,0:T(8,128)S(1)}, f32[128,512]{1,0:T(8,128)S(1)}, bf16[128,512]{1,0:T(8,128)(2,1)}, f32[64,512]{1,0:T(8,128)S(1)}) custom-call(s32[24]{0:T(128)S(1)} %concatenate.3.control, f32[128,512]{1,0:T(8,128)S(1)} %get-tuple-element.88.edge, f32[128,512]{1,0:T(8,128)S(1)} %get-tuple-element.89.inner, ...), custom_call_target="tpu_custom_call" | custom-call | tf_op jit(solution)/shard_map/inside_3_0/pallas_call | solution.py:27
  49.6 1.6 %outside_3_0.1 = (f32[128,512]{1,0:T(8,128)S(1)}, bf16[128,512]{1,0:T(8,128)(2,1)}, f32[5,8,1024]{2,1,0:T(8,128)S(1)}, f32[64,512]{1,0:T(8,128)S(1)}) custom-call(s32[24]{0:T(128)S(1)} %concatenate.3.control, f32[24]{0:T(128)S(1)} %reshape.20.weights, f32[128,512]{1,0:T(8,128)S(1)} %get-tuple-element.93.base, ...), custom_call_target="tpu_custom_call" | custom-call | tf_op jit(solution)/shard_map/outside_3_0/pallas_call | solution.py:27
  52.4 1.5 %inside_2_1.1 = (f32[64,512]{1,0:T(8,128)S(1)}, f32[64,512]{1,0:T(8,128)S(1)}, bf16[64,512]{1,0:T(8,128)(2,1)S(1)}, f32[64,512]{1,0:T(8,128)S(1)}, f32[64,512]{1,0:T(8,128)S(1)}) custom-call(s32[24]{0:T(128)S(1)} %concatenate.3.control, f32[64,512]{1,0:T(8,128)S(1)} %get-tuple-element.116.edge, f32[64,512]{1,0:T(8,128)S(1)} %get-tuple-element.117.inner, ...), custom_call_target="tpu_custom_call" | custom-call | tf_op jit(solution)/shard_map/inside_2_1/pallas_call | solution.py:27
  53.9 1.2 %collective-permute-start.25 = (bf16[64,512]{1,0:T(8,128)(2,1)S(1)}, bf16[64,512]{1,0:T(8,128)(2,1)S(1)}, u32[]{:S(2)}, u32[]{:S(2)}) collective-permute-start(bf16[64,512]{1,0:T(8,128)(2,1)S(1)} %get-tuple-element.123), channel_id=1, source_target_pairs={{0,1},{1,0},{2,3},{3,2},{4,5},{5,4},{6,7},{7,6},{8,9},{9,8},{10,11... | collective-permute-start | bytes 196616 | tf_op jit(solution)/shard_map/ppermute | solution.py:302
  56.7 1.4 %collective-permute-start.17 = (f32[64,512]{1,0:T(8,128)S(1)}, f32[64,512]{1,0:T(8,128)S(1)}, u32[]{:S(2)}, u32[]{:S(2)}) collective-permute-start(f32[64,512]{1,0:T(8,128)S(1)} %constant_dynamic-slice_fusion.1), channel_id=1, source_target_pairs={{0,1},{1,0},{2,3},{3,2},{4,5},{5,4},{6,7},{7,6},{8,9},{9,8},{10,11... | collective-permute-start | bytes 393224 | tf_op jit(solution)/shard_map/ppermute | solution.py:302
  58.2 1.8 %inside_3_1.1 = (f32[64,512]{1,0:T(8,128)S(1)}, f32[64,512]{1,0:T(8,128)S(1)}, bf16[64,512]{1,0:T(8,128)(2,1)}, f32[32,512]{1,0:T(8,128)S(1)}) custom-call(s32[24]{0:T(128)S(1)} %concatenate.3.control, f32[64,512]{1,0:T(8,128)S(1)} %get-tuple-element.121.edge, f32[64,512]{1,0:T(8,128)S(1)} %get-tuple-element.122.inner, ...), custom_call_target="tpu_custom_call" | custom-call | tf_op jit(solution)/shard_map/inside_3_1/pallas_call | solution.py:27
  60.5 1.4 %outside_3_1.1 = (f32[64,512]{1,0:T(8,128)S(1)}, bf16[64,512]{1,0:T(8,128)(2,1)}, f32[32,512]{1,0:T(8,128)S(1)}) custom-call(s32[24]{0:T(128)S(1)} %concatenate.3.control, f32[24]{0:T(128)S(1)} %reshape.20.weights, f32[64,512]{1,0:T(8,128)S(1)} %get-tuple-element.126.base, bf16[64,512]{1,0:T(8,128)(2,1)S(1)} %collective-permute-done.26.halo, ...), custom_call_target="tpu_custom_call" | custom-call | tf_op jit(solution)/shard_map/outside_3_1/pallas_call | solution.py:27
  65.0 1.9 %finish.1 = (f32[4,24,2048]{2,1,0:T(8,128)}, f32[4,24,2048]{2,1,0:T(8,128)}) custom-call(s32[24]{0:T(128)S(1)} %concatenate.3.control, f32[4,24,2048]{2,1,0:T(8,128)S(1)} %copy-done.3, f32[5,8,1024]{2,1,0:T(8,128)S(1)} %get-tuple-element.96.refs_1_, f32[5,8,1024]{2,1,0:T(8,128)S(1)} %collective-permute-done.12.refs_2_, ...), custom_call_target="tpu_custom_call" | custom-call | tf_op jit(solution)/shard_map/finish/pallas_call | solution.py:27
  (102 shorter events, 23.6 us)
Async XLA Ops:
  3.0 9.2 %collective-permute-start = (bf16[2,4,24,512]{3,2,1,0:T(8,128)(2,1)}, bf16[2,4,24,512]{3,2,1,0:T(8,128)(2,1)S(1)}, u32[]{:S(2)}, u32[]{:S(2)}) collective-permute-start(bf16[2,4,24,512]{3,2,1,0:T(8,128)(2,1)} %send_fraction.1), channel_id=1, source_target_pairs={{0,1},{1,0},{2,3},{3,2},{4,5},{5,4},{6,7},{7,6},{8,9},{9,8},{10,11... | collective-permute-start | bytes 589832 | tf_op jit(solution)/shard_map/ppermute | solution.py:302
  6.2 9.9 %collective-permute-start.2 = (f32[2,4,24,512]{3,2,1,0:T(8,128)S(1)}, f32[2,4,24,512]{3,2,1,0:T(8,128)S(1)}, u32[]{:S(2)}, u32[]{:S(2)}) collective-permute-start(f32[2,4,24,512]{3,2,1,0:T(8,128)S(1)} %send_drive.1), channel_id=1, source_target_pairs={{0,1},{1,0},{2,3},{3,2},{4,5},{5,4},{6,7},{7,6},{8,9},{9,8},{10,11... | collective-permute-start | bytes 1179656 | tf_op jit(solution)/shard_map/ppermute | solution.py:302
  13.0 7.4 %collective-permute-start.3 = (f32[5,8,1024]{2,1,0:T(8,128)S(1)}, f32[5,8,1024]{2,1,0:T(8,128)S(1)}, u32[]{:S(2)}, u32[]{:S(2)}) collective-permute-start(f32[5,8,1024]{2,1,0:T(8,128)S(1)} %get-tuple-element.72.rest_0_), channel_id=1, source_target_pairs={{0,2},{1,3},{2,0},{3,1},{4,6},{5,7},{6,4},{7,5},{8,10},{9,11},{10,... | collective-permute-start | bytes 491528 | tf_op jit(solution)/shard_map/ppermute | solution.py:316
  15.9 2.0 %collective-permute-start.1 = (bf16[128,512]{1,0:T(8,128)(2,1)S(1)}, bf16[128,512]{1,0:T(8,128)(2,1)S(1)}, u32[]{:S(2)}, u32[]{:S(2)}) collective-permute-start(bf16[128,512]{1,0:T(8,128)(2,1)S(1)} %get-tuple-element.69), channel_id=1, source_target_pairs={{0,1},{1,0},{2,3},{3,2},{4,5},{5,4},{6,7},{7,6},{8,9},{9,8},{10,11... | collective-permute-start | bytes 393224 | tf_op jit(solution)/shard_map/ppermute | solution.py:302
  15.9 5.9 %collective-permute-start.4 = (bf16[128,512]{1,0:T(8,128)(2,1)S(1)}, bf16[128,512]{1,0:T(8,128)(2,1)S(1)}, u32[]{:S(2)}, u32[]{:S(2)}) collective-permute-start(bf16[128,512]{1,0:T(8,128)(2,1)S(1)} %get-tuple-element.74.round_e), channel_id=1, source_target_pairs={{0,2},{1,4},{2,0},{3,6},{4,1},{5,8},{6,3},{7,10},{8,5},{9,12},{10,... | collective-permute-start | bytes 393224 | tf_op jit(solution)/shard_map/ppermute | solution.py:303
  21.6 2.8 %collective-permute-start.5 = (bf16[128,512]{1,0:T(8,128)(2,1)S(1)}, bf16[128,512]{1,0:T(8,128)(2,1)S(1)}, u32[]{:S(2)}, u32[]{:S(2)}) collective-permute-start(bf16[128,512]{1,0:T(8,128)(2,1)S(1)} %get-tuple-element.77), channel_id=1, source_target_pairs={{0,1},{1,0},{2,3},{3,2},{4,5},{5,4},{6,7},{7,6},{8,9},{9,8},{10,11... | collective-permute-start | bytes 393224 | tf_op jit(solution)/shard_map/ppermute | solution.py:302
  22.6 5.0 %collective-permute-start.6 = (bf16[128,512]{1,0:T(8,128)(2,1)S(1)}, bf16[128,512]{1,0:T(8,128)(2,1)S(1)}, u32[]{:S(2)}, u32[]{:S(2)}) collective-permute-start(bf16[128,512]{1,0:T(8,128)(2,1)S(1)} %get-tuple-element.81.round_e), channel_id=1, source_target_pairs={{0,2},{1,4},{2,0},{3,6},{4,1},{5,8},{6,3},{7,10},{8,5},{9,12},{10,... | collective-permute-start | bytes 393224 | tf_op jit(solution)/shard_map/ppermute | solution.py:303
  28.6 6.3 %collective-permute-start.8 = (f32[5,8,1024]{2,1,0:T(8,128)S(1)}, f32[5,8,1024]{2,1,0:T(8,128)S(1)}, u32[]{:S(2)}, u32[]{:S(2)}) collective-permute-start(f32[5,8,1024]{2,1,0:T(8,128)S(1)} %get-tuple-element.85.rest_0_), channel_id=1, source_target_pairs={{0,2},{1,3},{2,0},{3,1},{4,6},{5,7},{6,4},{7,5},{8,10},{9,11},{10,... | collective-permute-start | bytes 491528 | tf_op jit(solution)/shard_map/ppermute | solution.py:316
  30.4 2.6 %collective-permute-start.7 = (bf16[128,512]{1,0:T(8,128)(2,1)S(1)}, bf16[128,512]{1,0:T(8,128)(2,1)S(1)}, u32[]{:S(2)}, u32[]{:S(2)}) collective-permute-start(bf16[128,512]{1,0:T(8,128)(2,1)S(1)} %get-tuple-element.84), channel_id=1, source_target_pairs={{0,1},{1,0},{2,3},{3,2},{4,5},{5,4},{6,7},{7,6},{8,9},{9,8},{10,11... | collective-permute-start | bytes 393224 | tf_op jit(solution)/shard_map/ppermute | solution.py:302
  30.4 5.9 %collective-permute-start.9 = (bf16[128,512]{1,0:T(8,128)(2,1)S(1)}, bf16[128,512]{1,0:T(8,128)(2,1)S(1)}, u32[]{:S(2)}, u32[]{:S(2)}) collective-permute-start(bf16[128,512]{1,0:T(8,128)(2,1)S(1)} %get-tuple-element.87.round_e), channel_id=1, source_target_pairs={{0,2},{1,4},{2,0},{3,6},{4,1},{5,8},{6,3},{7,10},{8,5},{9,12},{10,... | collective-permute-start | bytes 393224 | tf_op jit(solution)/shard_map/ppermute | solution.py:303
  30.7 8.2 %collective-permute-start.19 = (bf16[64,512]{1,0:T(8,128)(2,1)S(1)}, bf16[64,512]{1,0:T(8,128)(2,1)S(1)}, u32[]{:S(2)}, u32[]{:S(2)}) collective-permute-start(bf16[64,512]{1,0:T(8,128)(2,1)S(1)} %get-tuple-element.104), channel_id=1, source_target_pairs={{0,1},{1,0},{2,3},{3,2},{4,5},{5,4},{6,7},{7,6},{8,9},{9,8},{10,11... | collective-permute-start | bytes 196616 | tf_op jit(solution)/shard_map/ppermute | solution.py:302
  32.5 7.9 %collective-permute-start.20 = (bf16[64,512]{1,0:T(8,128)(2,1)S(1)}, bf16[64,512]{1,0:T(8,128)(2,1)S(1)}, u32[]{:S(2)}, u32[]{:S(2)}) collective-permute-start(bf16[64,512]{1,0:T(8,128)(2,1)S(1)} %get-tuple-element.108.round_e), channel_id=1, source_target_pairs={{0,2},{1,4},{2,0},{3,6},{4,1},{5,8},{6,3},{7,10},{8,5},{9,12},{10,... | collective-permute-start | bytes 196616 | tf_op jit(solution)/shard_map/ppermute | solution.py:303
  36.1 11.8 %collective-permute-start.10 = (bf16[128,512]{1,0:T(8,128)(2,1)S(1)}, bf16[128,512]{1,0:T(8,128)(2,1)S(1)}, u32[]{:S(2)}, u32[]{:S(2)}) collective-permute-start(bf16[128,512]{1,0:T(8,128)(2,1)S(1)} %get-tuple-element.90), channel_id=1, source_target_pairs={{0,1},{1,0},{2,3},{3,2},{4,5},{5,4},{6,7},{7,6},{8,9},{9,8},{10,11... | collective-permute-start | bytes 393224 | tf_op jit(solution)/shard_map/ppermute | solution.py:302
  37.1 12.5 %collective-permute-start.11 = (bf16[128,512]{1,0:T(8,128)(2,1)S(1)}, bf16[128,512]{1,0:T(8,128)(2,1)S(1)}, u32[]{:S(2)}, u32[]{:S(2)}) collective-permute-start(bf16[128,512]{1,0:T(8,128)(2,1)S(1)} %get-tuple-element.94.round_e), channel_id=1, source_target_pairs={{0,2},{1,4},{2,0},{3,6},{4,1},{5,8},{6,3},{7,10},{8,5},{9,12},{10,... | collective-permute-start | bytes 393224 | tf_op jit(solution)/shard_map/ppermute | solution.py:303
  40.1 2.7 %collective-permute-start.21 = (bf16[64,512]{1,0:T(8,128)(2,1)S(1)}, bf16[64,512]{1,0:T(8,128)(2,1)S(1)}, u32[]{:S(2)}, u32[]{:S(2)}) collective-permute-start(bf16[64,512]{1,0:T(8,128)(2,1)S(1)} %get-tuple-element.111), channel_id=1, source_target_pairs={{0,1},{1,0},{2,3},{3,2},{4,5},{5,4},{6,7},{7,6},{8,9},{9,8},{10,11... | collective-permute-start | bytes 196616 | tf_op jit(solution)/shard_map/ppermute | solution.py:302
  41.2 4.3 %collective-permute-start.22 = (bf16[64,512]{1,0:T(8,128)(2,1)S(1)}, bf16[64,512]{1,0:T(8,128)(2,1)S(1)}, u32[]{:S(2)}, u32[]{:S(2)}) collective-permute-start(bf16[64,512]{1,0:T(8,128)(2,1)S(1)} %get-tuple-element.115.round_e), channel_id=1, source_target_pairs={{0,2},{1,4},{2,0},{3,6},{4,1},{5,8},{6,3},{7,10},{8,5},{9,12},{10,... | collective-permute-start | bytes 196616 | tf_op jit(solution)/shard_map/ppermute | solution.py:303
  44.5 7.9 %collective-permute-start.23 = (bf16[64,512]{1,0:T(8,128)(2,1)}, bf16[64,512]{1,0:T(8,128)(2,1)}, u32[]{:S(2)}, u32[]{:S(2)}) collective-permute-start(bf16[64,512]{1,0:T(8,128)(2,1)} %get-tuple-element.118), channel_id=1, source_target_pairs={{0,1},{1,0},{2,3},{3,2},{4,5},{5,4},{6,7},{7,6},{8,9},{9,8},{10,11... | collective-permute-start | bytes 196616 | tf_op jit(solution)/shard_map/ppermute | solution.py:302
  46.3 8.8 %collective-permute-start.24 = (bf16[64,512]{1,0:T(8,128)(2,1)S(1)}, bf16[64,512]{1,0:T(8,128)(2,1)}, u32[]{:S(2)}, u32[]{:S(2)}) collective-permute-start(bf16[64,512]{1,0:T(8,128)(2,1)S(1)} %get-tuple-element.120.round_e), channel_id=1, source_target_pairs={{0,2},{1,4},{2,0},{3,6},{4,1},{5,8},{6,3},{7,10},{8,5},{9,12},{10,... | collective-permute-start | bytes 196616 | tf_op jit(solution)/shard_map/ppermute | solution.py:303
  51.9 10.5 %collective-permute-start.12 = (f32[5,8,1024]{2,1,0:T(8,128)S(1)}, f32[5,8,1024]{2,1,0:T(8,128)S(1)}, u32[]{:S(2)}, u32[]{:S(2)}) collective-permute-start(f32[5,8,1024]{2,1,0:T(8,128)S(1)} %get-tuple-element.96.refs_1_), channel_id=1, source_target_pairs={{0,2},{1,3},{2,0},{3,1},{4,6},{5,7},{6,4},{7,5},{8,10},{9,11},{10,... | collective-permute-start | bytes 491528 | tf_op jit(solution)/shard_map/ppermute | solution.py:316
  53.9 4.3 %collective-permute-start.25 = (bf16[64,512]{1,0:T(8,128)(2,1)S(1)}, bf16[64,512]{1,0:T(8,128)(2,1)S(1)}, u32[]{:S(2)}, u32[]{:S(2)}) collective-permute-start(bf16[64,512]{1,0:T(8,128)(2,1)S(1)} %get-tuple-element.123), channel_id=1, source_target_pairs={{0,1},{1,0},{2,3},{3,2},{4,5},{5,4},{6,7},{7,6},{8,9},{9,8},{10,11... | collective-permute-start | bytes 196616 | tf_op jit(solution)/shard_map/ppermute | solution.py:302
  56.1 4.3 %collective-permute-start.26 = (bf16[64,512]{1,0:T(8,128)(2,1)S(1)}, bf16[64,512]{1,0:T(8,128)(2,1)S(1)}, u32[]{:S(2)}, u32[]{:S(2)}) collective-permute-start(bf16[64,512]{1,0:T(8,128)(2,1)S(1)} %get-tuple-element.127.round_e), channel_id=1, source_target_pairs={{0,2},{1,4},{2,0},{3,6},{4,1},{5,8},{6,3},{7,10},{8,5},{9,12},{10,... | collective-permute-start | bytes 196616 | tf_op jit(solution)/shard_map/ppermute | solution.py:303
  56.7 6.9 %collective-permute-start.17 = (f32[64,512]{1,0:T(8,128)S(1)}, f32[64,512]{1,0:T(8,128)S(1)}, u32[]{:S(2)}, u32[]{:S(2)}) collective-permute-start(f32[64,512]{1,0:T(8,128)S(1)} %constant_dynamic-slice_fusion.1), channel_id=1, source_target_pairs={{0,1},{1,0},{2,3},{3,2},{4,5},{5,4},{6,7},{7,6},{8,9},{9,8},{10,11... | collective-permute-start | bytes 393224 | tf_op jit(solution)/shard_map/ppermute | solution.py:302
  62.4 2.6 %collective-permute-start.13 = (f32[5,8,1024]{2,1,0:T(8,128)S(1)}, f32[5,8,1024]{2,1,0:T(8,128)S(1)}, u32[]{:S(2)}, u32[]{:S(2)}) collective-permute-start(f32[5,8,1024]{2,1,0:T(8,128)S(1)} %get-tuple-element.96.refs_1_), channel_id=1, source_target_pairs={{0,1},{1,0},{2,3},{3,2},{4,5},{5,4},{6,7},{7,6},{8,9},{9,8},{10,11... | collective-permute-start | bytes 491528 | tf_op jit(solution)/shard_map/ppermute | solution.py:302
  62.4 2.6 %collective-permute-start.14 = (f32[5,8,1024]{2,1,0:T(8,128)S(1)}, f32[5,8,1024]{2,1,0:T(8,128)S(1)}, u32[]{:S(2)}, u32[]{:S(2)}) collective-permute-start(f32[5,8,1024]{2,1,0:T(8,128)S(1)} %collective-permute-done.12.refs_2_), channel_id=1, source_target_pairs={{0,1},{1,0},{2,3},{3,2},{4,5},{5,4},{6,7},{7,6},{8,9},{9,8},{10,11... | collective-permute-start | bytes 491528 | tf_op jit(solution)/shard_map/ppermute | solution.py:302
  (20 other events, 82.7 us)

commit v2 on v0

v2 whole, which is shorter than its diff:
```python
import functools
import jax
import jax.numpy as jnp
from jax import lax
from jax.experimental import pallas as pl
from jax.experimental.pallas import tpu as pltpu
from jax.sharding import PartitionSpec as P

TILE = 512
SECTIONS = 4
NODES1 = 4
NODES2 = 16
ITERS = 2
PG_STEPS = 2
SUB = 8
AXES = ("space", "scen")
CHAINS = ((0, 24),)
HALF = 0.5
VMEM_LIMIT = 8 << 20

f32, bf16 = jnp.float32, jnp.bfloat16
HBM = pl.BlockSpec(memory_space=pltpu.HBM)
VMEM = pl.BlockSpec(memory_space=pltpu.VMEM)
LANE = 128
SLOT_IN, SLOT_OUT, END, SLOT_EDGE, SLOT_OTHER = range(5)


def call(kernel, arrays, out, far=(), scratch=(), after=()):
    held = len(far) + len(arrays)

    def body(*refs):
        kernel(*refs[:held], *refs[held + len(after) :])

    return pl.pallas_call(
        body,
        out_shape=[jax.ShapeDtypeStruct(s, d) for s, d in out],
        in_specs=[HBM] * len(far) + [VMEM] * (len(arrays) + len(after)),
        out_specs=[VMEM] * len(out),
        scratch_shapes=list(scratch),
        compiler_params=pltpu.CompilerParams(vmem_limit_bytes=VMEM_LIMIT),
    )(*(pltpu.with_memory_space_constraint(x, pltpu.HBM) for x in far), *arrays, *after)


def lanes(tile):
    return pl.ds(pl.multiple_of(tile * TILE, TILE), TILE)


class Plan:
    def __init__(self, mesh, fraction, cone_list, node_list):
        self.spaces, self.scens = mesh.shape["space"], mesh.shape["scen"]
        self.rank, self.periods, width = fraction.shape
        self.tiles = cone_list.shape[0]
        self.quarter = self.periods // SECTIONS
        self.local = 2 * self.rank
        self.total = node_list.shape[1]
        self.second = self.total > NODES2
        self.blocks = 1 + NODES1 + (NODES2 if self.second else 0)
        self.reach = (3 if self.second else 2) * self.quarter
        self.groups = -(-self.reach // SUB)
        self.chains = CHAINS

    def averaged(self, chain):
        return chain[0] < self.reach

    def section_of(self, block):
        return 0 if block == 0 else 1 if block <= NODES1 else 2

    def meets(self, low, section):
        return low < (section + 1) * self.quarter and low + SUB > section * self.quarter

    def blocks_at(self, low):
        return [b for b in range(self.blocks) if self.meets(low, self.section_of(b))]

    def core(self):
        return lax.axis_index("scen") % 2

    def edge_of(self, core):
        return core * (self.tiles - 1)

    def inner_of(self, core):
        return 1 + core * (self.tiles - 3)


def rows_from(start, count):
    return pl.ds(pl.multiple_of(start, SUB), count)


def prepare_kernel(plan, *refs):
    small_far, (start, ore, dual) = refs[:3], refs[3:6]
    held, drive, drive_sent, control, share, select = refs[6:12]
    ores, duals, *small, sems = refs[12:]
    core = plan.core()
    copies = []
    for source, target in zip(small_far, small):
        copies.append(pltpu.make_async_copy(source, target, sems.at[len(copies)]))
    for k in range(2):
        for which, at in enumerate((core, 1 - core)):
            tile = (plan.edge_of, plan.inner_of)[k](at)
            fetch = [(ore, ores.at[which, k]), (dual, duals.at[which, k])] + ([(start, held.at[k])] if which == 0 else [])
            for source, target in fetch:
                copies.append(pltpu.make_async_copy(source.at[:, :, lanes(tile)], target, sems.at[len(copies)]))
    for copy in copies:
        copy.start()
    for copy in copies[: len(small)]:
        copy.wait()
    cones, nodes, chances = small
    edge, inner = plan.edge_of(core), plan.inner_of(core)
    base = lax.axis_index("space") * plan.tiles
    slot_in = jnp.where(cones[edge, 1] == base + inner, 1, 2)
    slot_out = 3 - slot_in
    end = jnp.where(cones[edge, slot_out] == base + edge, 1, 0)
    slot_edge = jnp.where(cones[inner, 1] == base + edge, 1, 2)
    place = lax.broadcasted_iota(jnp.int32, (SUB, LANE), 1)
    vector = jnp.zeros((SUB, LANE), jnp.int32)
    for k, v in enumerate((slot_in, slot_out, end, slot_edge, 3 - slot_edge)):
        vector = jnp.where(place == k, v, vector)
    control[...] = vector
    first = (lax.axis_index("scen") // 2) * plan.local
    splat = lambda v: jnp.full((SUB, LANE), v, f32)
    sections = 3 if plan.second else 2
    for j in range(plan.local):
        mine = first + j
        weights = []
        for section in range(sections):
            total = jnp.float32(0)
            for other in range(plan.total):
                chance = chances[other]
                if section:
                    chance = jnp.where(nodes[section - 1, other] == nodes[section - 1, mine], chance, 0.0)
                total = total + chance
            weights.append(splat(chances[mine]) / splat(total))
        for group in range(plan.groups):
            period = group * SUB + lax.broadcasted_iota(jnp.int32, (SUB, LANE), 0)
            for block in plan.blocks_at(group * SUB):
                section = plan.section_of(block)
                inside = (period >= section * plan.quarter) & (period < (section + 1) * plan.quarter)
                chosen = jnp.where(inside, 1.0, 0.0)
                if section:
                    node = block - (1 if section == 1 else 1 + NODES1)
                    chosen = chosen * jnp.where(nodes[section - 1, mine] == node, 1.0, 0.0)
                select[group, block, j] = chosen
                share[group, block, j] = chosen * weights[section]
    for copy in copies[len(small) :]:
        copy.wait()
    for k in range(2):
        drive[k] = ores[0, k].astype(f32) - duals[0, k]
        drive_sent[k] = ores[1, k].astype(f32) - duals[1, k]


def means_of_tile(plan, chain, share, source, sums, sent):
    lo, hi = chain
    size = hi - lo
    for chunk in range(TILE // LANE):
        span = slice(chunk * LANE, (chunk + 1) * LANE)
        totals = [jnp.zeros((SUB, LANE), f32)] * plan.blocks
        for low in range(lo, min(hi, plan.reach), SUB):
            for j in range(plan.local):
                row = j * size + low - lo
                value = source[row : row + SUB, span] - HALF
                for block in plan.blocks_at(low):
                    totals[block] = totals[block] + share[low // SUB, block, j] * value
        for block in range(plan.blocks):
            sums[block, :, span] = totals[block]
            sent[block, :, span] = totals[block].astype(bf16)


def means_kernel(plan, chain, final, share, *refs):
    count = (len(refs) - final) // 3
    for k in range(count):
        means_of_tile(plan, chain, share, refs[k], refs[count + k], refs[2 * count + k])
    if final:
        source, sums, packed = refs[0], refs[1], refs[-1]
        rows = plan.rank * (chain[1] - chain[0])
        packed[:rows, :] = other_rows(plan, chain, source)
        for block in range(plan.blocks):
            packed[rows + block * SUB : rows + (block + 1) * SUB, :] = sums[block]


def whole_means(plan, pair, span):
    return [pair[0][b, :, span] + pair[1][b, :, span].astype(f32) + HALF for b in range(plan.blocks)]


def center_rows(plan, low, j, select, means, value):
    if low >= plan.reach:
        return value
    mean = jnp.zeros_like(value)
    for block in plan.blocks_at(low):
        mean = mean + select[low // SUB, block, j] * means[block]
    if low + SUB > plan.reach:
        period = low + lax.broadcasted_iota(jnp.int32, value.shape, 0)
        mean = jnp.where(period < plan.reach, mean, value)
    return mean


def assemble(plan, own, theirs, out):
    core = plan.core()
    for (lo, hi), pair in zip(plan.chains, out):
        size = hi - lo
        for k, ref in enumerate(pair):
            for r in range(plan.rank):
                ref[rows_from((core * plan.rank + r) * size, size), :] = own(k, r, lo, hi).astype(f32)
                ref[rows_from(((1 - core) * plan.rank + r) * size, size), :] = theirs(k, r, lo, hi).astype(f32)


def start_kernel(plan, held, came, *outs):
    n = len(plan.chains)
    state = [outs[2 * c : 2 * c + 2] for c in range(n)]
    sends = [outs[2 * n + 2 * c : 2 * n + 2 * c + 2] for c in range(n)]
    tiles = (plan.edge_of(plan.core()), plan.inner_of(plan.core()))
    assemble(plan, lambda k, r, lo, hi: held[k, r, lo:hi, :], lambda k, r, lo, hi: came[r, lo:hi, lanes(tiles[k])], state)
    for pair, send in zip(state, sends):
        for ref, out in zip(pair, send):
            out[...] = ref[...].astype(bf16)


def drive_kernel(plan, held, came, *outs):
    take = lambda ref: lambda k, r, lo, hi: ref[k, r, lo:hi, :]
    assemble(plan, take(held), take(came), [outs[2 * c : 2 * c + 2] for c in range(len(plan.chains))])


def other_rows(plan, chain, ref):
    count = plan.rank * (chain[1] - chain[0])
    return ref[rows_from((1 - plan.core()) * count, count), :]


def inside_kernel(plan, chain, first, last_round, final, control, edge, inner, halo, drive_e, drive_n, patterns, *rest):
    lo, hi = chain
    size = hi - lo
    averaged = plan.averaged(chain)
    rest = list(rest)
    pull_e, pull_n = drive_e, drive_n
    if first and averaged:
        select = rest.pop(0)
        means_refs = [(rest.pop(0), rest.pop(0)) for _ in range(2)]
    base_e, next_n = rest[:2]
    rest = rest[2:]
    if not final:
        send_n = rest.pop(0)
    if first:
        pull_e, pull_n = rest[:2]
        rest = rest[2:]
        moved = rest[:3] if last_round and averaged else None
        for side, (value, drive, pull) in enumerate(((edge, drive_e, pull_e), (inner, drive_n, pull_n))):
            if not averaged:
                pull[...] = drive[...] + value[...]
                continue
            for chunk in range(TILE // LANE):
                span = slice(chunk * LANE, (chunk + 1) * LANE)
                means = whole_means(plan, means_refs[side], span)
                for j in range(plan.local):
                    for low in range(lo, hi, SUB):
                        rows = slice(j * size + low - lo, j * size + low - lo + SUB)
                        now = value[rows, span]
                        mean = center_rows(plan, low, j, select, means, now)
                        if last_round:
                            gap = now - mean
                            moved[side][rows, span] = gap
                            pull[rows, span] = drive[rows, span] - gap + mean
                        else:
                            pull[rows, span] = drive[rows, span] + mean
        if moved:
            for side in range(2):
                moved[2][side] = other_rows(plan, chain, moved[side])
    round_e, round_n = edge[...].astype(bf16), inner[...].astype(bf16)
    dot = functools.partial(jnp.dot, preferred_element_type=f32)
    cone = dot(round_n, patterns[0]) + dot(round_e, patterns[control[0, SLOT_EDGE]]) + dot(halo[...], patterns[control[0, SLOT_OTHER]])
    value = inner[...]
    value = jnp.clip(value - 0.4 * ((value - cone) + value - pull_n[...]), 0.0, 1.0)
    next_n[...] = value
    if not final:
        send_n[...] = value.astype(bf16)
    cone = dot(round_e, patterns[0]) + dot(round_n, patterns[control[0, SLOT_IN]])
    value = edge[...]
    base_e[...] = value - 0.4 * ((value - cone) + value - pull_e[...])

    @pl.when(control[0, END] == 1)
    def _():
        base_e[...] += 0.4 * dot(round_e, patterns[control[0, SLOT_OUT]])


def outside_kernel(plan, control, base, halo, patterns, next_e, send_e=None):
    scale = 0.4 * (1 - control[0, END]).astype(f32)
    cone = jnp.dot(halo[...], patterns[control[0, SLOT_OUT]], preferred_element_type=f32)
    value = jnp.clip(base[...] + scale * cone, 0.0, 1.0)
    next_e[...] = value
    if send_e is not None:
        send_e[...] = value.astype(bf16)


def front_kernel(plan, dual, *refs):
    refs = list(refs)
    fraction, price = refs[-2:]
    core = plan.core()
    tiles = [(plan.edge_of(c), plan.inner_of(c)) for c in (core, 1 - core)]
    at = 0
    for lo, hi in plan.chains:
        size = hi - lo
        held, came = refs[at : at + 2], refs[at + 2 : at + 4]
        at += 4
        averaged = plan.averaged((lo, hi))
        if averaged:
            moved, moved_came = refs[at : at + 2], refs[at + 2]
            at += 3
        for part in range(2):
            for side in range(2):
                for r in range(plan.rank):
                    if part == 0:
                        rows, value, gap = rows_from((core * plan.rank + r) * size, size), held[side], averaged and moved[side]
                    else:
                        rows, value, gap = slice(r * size, (r + 1) * size), came[side], averaged and moved_came.at[side]
                    out = (r, slice(lo, hi), lanes(tiles[part][side]))
                    now, first = value[rows, :], dual[out]
                    fraction[out] = now
                    if averaged:
                        period = lo + lax.broadcasted_iota(jnp.int32, now.shape, 0)
                        first = jnp.where(period < plan.reach, first + gap[rows, :] + now, first)
                    price[out] = first


def finish_kernel(plan, offset, price, select, *refs):
    pairs = [[(refs[4 * p + 2 * s], refs[4 * p + 2 * s + 1]) for s in range(2)] for p in range(2)]
    out = refs[-1]
    core = plan.core()
    tiles = [(plan.edge_of(c), plan.inner_of(c)) for c in (core, 1 - core)]
    top = plan.groups * SUB
    if top < plan.periods:
        out[:, top:, :] = price[:, top:, :]
    for part in range(2):
        for side in range(2):
            for chunk in range(TILE // LANE):
                span = slice(chunk * LANE, (chunk + 1) * LANE)
                first, second = pairs[part][side]
                if part and offset:
                    first = [first[offset + b * SUB : offset + (b + 1) * SUB, span] for b in range(plan.blocks)]
                    means = [first[b] + second[b, :, span].astype(f32) + HALF for b in range(plan.blocks)]
                else:
                    means = whole_means(plan, (first, second), span)
                where = pl.ds(pl.multiple_of(tiles[part][side] * TILE + chunk * LANE, LANE), LANE)
                for r in range(plan.rank):
                    for low in range(0, top, SUB):
                        value = price[r, low : low + SUB, where]
                        for block in plan.blocks_at(low):
                            value = value - select[low // SUB, block, core * plan.rank + r] * means[block]
                        out[r, low : low + SUB, where] = value


def partners(plan):
    pairs = []
    for i in range(plan.spaces):
        for s in range(plan.scens):
            to = i + 1 if s % 2 else i - 1
            if 0 <= to < plan.spaces:
                pairs.append((i * plan.scens + s, to * plan.scens + (s ^ 1)))
            else:
                pairs.append((i * plan.scens + s, i * plan.scens + (s ^ 2 if plan.scens % 4 == 0 else s)))
    return pairs


def tiled(plan, start, ore, dual, patterns, cone_list, node_list, probability):
    flip = [(i, i ^ 1) for i in range(plan.scens)]
    edges = partners(plan)

    swap = lambda x: lax.ppermute(x, "scen", flip)
    outer = lambda x: lax.ppermute(x, AXES, edges)
    half = (2, plan.rank, plan.periods, TILE)
    sums = (plan.blocks, SUB, TILE)
    shares = (plan.groups, plan.blocks, plan.local, SUB, LANE)
    chains = plan.chains
    n = len(chains)
    rows = [plan.local * (hi - lo) for lo, hi in chains]
    part = lambda f, *a: functools.partial(f, plan, *a)
    ranks = range(n)
    pairs = lambda kind: [((r, TILE), kind) for r in rows for _ in range(2)]
    bits = [1 << b for b in range(1, plan.scens.bit_length() - 1)]
    jump = lambda x, bit: lax.ppermute(x, "scen", [(i, i ^ bit) for i in range(plan.scens)])

    def across(x, sent):
        other = None
        for k, bit in enumerate(bits):
            if k:
                x = x + other.astype(f32)
                sent = x.astype(bf16)
            other = jump(sent, bit)
        return x, (jnp.zeros_like(sent) if other is None else other), sent

    def means_of(sides, final=False, after=()):
        count = len(sides)
        total = None
        for c in ranks:
            if plan.averaged(chains[c]):
                arrays = [share, *(state[c][k] for k in sides)]
                outs = [(sums, f32)] * count + [(sums, bf16)] * count
                outs += [((plan.rank * (chains[c][1] - chains[c][0]) + plan.blocks * SUB, TILE), f32)] if final else []
                got = call(part(means_kernel, chains[c], final), arrays, outs, after=after)
                got = list(got)
                if final:
                    sent[c][sides[0]] = got.pop()
                if total is not None:
                    got = [g + t for g, t in zip(got[:count], total)]
                    got += [g.astype(bf16) for g in got]
                total = got
        return [across(total[k], total[count + k]) for k in range(count)]

    came = swap(start)
    parts = (2, 2, plan.rank, plan.periods, TILE)
    held, drive_held, drive_sent, control, share, select = call(
        part(prepare_kernel), [],
        [(half, bf16), (half, f32), (half, f32), ((SUB, LANE), jnp.int32), (shares, f32), (shares, f32)],
        far=[cone_list, node_list, probability, start, ore, dual],
        scratch=[
            pltpu.VMEM(parts, bf16),
            pltpu.VMEM(parts, f32),
            *(pltpu.SMEM(x.shape, x.dtype) for x in (cone_list, node_list, probability)),
            pltpu.SemaphoreType.DMA((13,)),
        ],
    )
    got = call(part(start_kernel), [held, came], pairs(f32) + pairs(bf16))
    state = [list(got[2 * c : 2 * c + 2]) for c in ranks]
    rounded = [list(got[2 * n + 2 * c : 2 * n + 2 * c + 2]) for c in ranks]
    halo = [[outer(rounded[c][0]), swap(rounded[c][1])] for c in ranks]
    means = means_of((0, 1))
    drive_came = swap(drive_sent)
    got = call(part(drive_kernel), [drive_held, drive_came], pairs(f32))
    drive = [list(got[2 * c : 2 * c + 2]) for c in ranks]
    moved, pull = [None] * n, [None] * n
    sent = [[None, None] for _ in ranks]
    last = []
    for step in range(ITERS * PG_STEPS):
        first = step % PG_STEPS == 0
        closing = step % PG_STEPS == PG_STEPS - 1
        final = step == ITERS * PG_STEPS - 1
        last_round = step >= PG_STEPS
        base, halo_n = [None] * n, [None] * n
        order = sorted(ranks, key=lambda c: first and plan.averaged(chains[c]))
        for c in order:
            chain = chains[c]
            averaged = plan.averaged(chain)
            shape = (rows[c], TILE)
            quart = (2, plan.rank * (chain[1] - chain[0]), TILE)
            arrays = [control, *state[c], halo[c][1], *(drive if first else pull)[c], patterns]
            outs = [(shape, f32), (shape, f32)] + ([] if final else [(shape, bf16)])
            if first:
                arrays += [select, *means[0][:2], *means[1][:2]] if averaged else []
                outs += [(shape, f32)] * 2
                outs += [(shape, f32)] * 2 + [(quart, f32)] if last_round and averaged else []
            got = call(part(inside_kernel, chain, first, last_round, final), arrays, outs, after=last)
            last = [got[0]]
            base[c], state[c][1] = got[:2]
            if first:
                pull[c] = list(got[3:5])
                if last_round and averaged:
                    moved[c] = [*got[5:7], swap(got[7])]
            if not final:
                halo_n[c] = swap(got[2])
        if closing:
            means_n = means_of((1,), final)
            last = [means_n[0][2]]
        for c in ranks:
            chain = chains[c]
            shape = (rows[c], TILE)
            outs = [(shape, f32)] + ([] if final else [(shape, bf16)])
            got = call(part(outside_kernel), [control, base[c], halo[c][0], patterns], outs, after=last)
            last = [got[0]]
            state[c][0] = got[0]
            if not final:
                halo[c] = [outer(got[1]), halo_n[c]]
            if closing and c == max(k for k in ranks if plan.averaged(chains[k])):
                means = means_of((0,), final) + means_n
    averaged = [c for c in ranks if plan.averaged(chains[c])]
    packed = len(averaged) == 1 and len(bits) == 1
    for c in ranks:
        if plan.averaged(chains[c]):
            sent[c] = [swap(x) for x in sent[c]]
        else:
            count = plan.rank * (chains[c][1] - chains[c][0])
            sent[c] = [swap(call(lambda x, o, c=c: o.__setitem__(..., other_rows(plan, chains[c], x)), [x], [((count, TILE), f32)])[0]) for x in state[c]]
    theirs = [(sent[averaged[0]][k] if packed else swap(means[k][0]), swap(means[k][1])) for k in range(2)]
    arrays = [dual]
    for c in ranks:
        arrays += state[c] + sent[c] + (moved[c] if plan.averaged(chains[c]) else [])
    fraction, price = call(part(front_kernel), arrays, [(start.shape, f32)] * 2)
    arrays = [price, select, *means[0][:2], *means[1][:2], *theirs[0], *theirs[1]]
    offset = plan.rank * (chains[averaged[0]][1] - chains[averaged[0]][0]) if packed else 0
    return fraction, call(part(finish_kernel, offset), arrays, [(start.shape, f32)])[0]


def solution(mesh):
    def body(start, ore, dual, patterns, cone_list, node_list, probability):
        plan = Plan(mesh, start, cone_list, node_list)
        assert plan.tiles == 4 and plan.scens % 2 == 0 and plan.periods % SUB == 0
        return tiled(plan, start, ore, dual, patterns, cone_list, node_list, probability)

    split = P("scen", None, "space")
    in_specs = (split, split, split, P(), P("space", None), P(), P())
    return jax.shard_map(body, mesh=mesh, in_specs=in_specs, out_specs=(split, split), check_vma=False)
```

time: 305 us -> 44.2 us (0.14)
  local copies, waits for them, and re-layouts: 107 us -> 0.01 us
  other arithmetic: 45.4 us -> 0 us
  blocking collectives: 35.9 us -> 0 us
  waiting for transfers between devices: 48.7 us -> 14.9 us
  matrix products: 27.5 us -> 0 us
  between operations: 14.6 us -> 0.82 us
  Pallas kernels: 0 us -> 11.3 us
  starting transfers between devices: 22.5 us -> 17 us
    psum x3 -> x0, waiting for transfers between devices: 40.1 us -> none  [tree_center(): lax.psum((root_term, first_term, second_term), 'scen')]
    gather x18 -> x0, local copies, waits for them, and re-layouts: 38.2 us -> none  [the longest x12 23.2 us: descend(): jnp.take(extended, local_cone[:, cone_slot], axis=2).reshape(-1, TILE)]
    psum x3 -> x0, blocking collectives: 35.9 us -> none  [tree_center(): lax.psum((root_term, first_term, second_term), 'scen')]
    reshape x20 -> x0, local copies, waits for them, and re-layouts: 28.6 us -> none  [the longest x12 13.9 us: descend(): jnp.take(extended, local_cone[:, cone_slot], axis=2).reshape(-1, TILE)]
    dot_general x21 -> x0, matrix products: 27.5 us -> none  [the longest x12 16.7 us: descend(): jnp.dot(picked, patterns[cone_slot], preferred_element_type=jnp.float32)]
    select_n x20 -> x0, other arithmetic: 15.2 us -> none  [the longest x14 7.88 us: descend(): jnp.take(extended, local_cone[:, cone_slot], axis=2).reshape(-1, TILE)]
    unnamed x98 -> x4, local copies, waits for them, and re-layouts: 12.5 us -> 0.01 us
    convert_element_type x3 -> x0, other arithmetic: 11.6 us -> none  [descend(): rounded = fraction.astype(jnp.bfloat16)]
  transfers between devices with their start and end apart: 11 -> 21, of which waited for: 8 -> 9; matrix products, arithmetic and copies ran while one was open for 20% -> 0% of each run, Pallas kernels for 0% -> 23%
where the time goes in v2:
time: 44.2 us; the launch traced here: 44.1 us
  starting transfers between devices  17 us (38%)
  waiting for transfers between devices  14.9 us (34%)
  Pallas kernels  11.3 us (26%)
  between operations  0.82 us (2%)
    pallas_call x18, Pallas kernels, call(): pl.pallas_call(body, out_shape=[jax.ShapeDtypeStruct(s, d) for s, d in ou...  11.3 us
    ppermute x6, waiting for transfers between devices, tiled(): lax.ppermute(x, 'scen', [(i, i ^ bit) for i in range(plan.scens)])  10.2 us
    ppermute x4, starting transfers between devices, tiled(): outer = lambda x: lax.ppermute(x, AXES, edges)  8.81 us
    ppermute x6, starting transfers between devices, tiled(): lax.ppermute(x, 'scen', [(i, i ^ bit) for i in range(plan.scens)])  6.23 us
    ppermute x4, waiting for transfers between devices, tiled(): outer = lambda x: lax.ppermute(x, AXES, edges)  4.55 us
    ppermute x11, starting transfers between devices, tiled(): swap = lambda x: lax.ppermute(x, 'scen', flip)  1.99 us
  transfers between devices with their start and end apart: 21, of which 9 were waited for; matrix products, arithmetic and copies ran while one was open for 0% of the time, Pallas kernels for 23%

profile of v2, /device:TPU:0, one launch (start us, length us, event | category | flops | bytes accessed | tf_op | source)
XLA Modules:
  0.0 44.1 jit_solution(2810268012150103117)
XLA Ops:
  0.6 0.6 %collective-permute-start = (bf16[4,24,2048]{2,1,0:T(8,128)(2,1)}, bf16[4,24,2048]{2,1,0:T(8,128)(2,1)S(1)}, u32[]{:S(2)}, u32[]{:S(2)}) collective-permute-start(bf16[4,24,2048]{2,1,0:T(8,128)(2,1)} %refs_3_.5), channel_id=1, source_target_pairs={{0,1},{1,0},{2,3},{3,2},{4,5},{5,4},{6,7},{7,6},{8,9},{9,8},{10,11... | collective-permute-start | bytes 1179656 | tf_op jit(solution)/shard_map/ppermute | solution.py:363
  1.2 1.6 %shard_map.86 = (bf16[2,4,24,512]{3,2,1,0:T(8,128)(2,1)S(1)}, f32[2,4,24,512]{3,2,1,0:T(8,128)S(1)}, f32[2,4,24,512]{3,2,1,0:T(8,128)S(1)}, s32[8,128]{1,0:T(8,1...) custom-call(s32[4,3]{1,0:T(4,128)} %refs_0_.2, s32[2,16]{1,0:T(2,128)} %refs_1_.1, ...), custom_call_target="tpu_custom_call" | custom-call | tf_op jit(solution)/shard_map/pallas_call | solution.py:34
  3.0 0.5 %collective-permute-start.1 = (bf16[192,512]{1,0:T(8,128)(2,1)S(1)}, bf16[192,512]{1,0:T(8,128)(2,1)S(1)}, u32[]{:S(2)}, u32[]{:S(2)}) collective-permute-start(bf16[192,512]{1,0:T(8,128)(2,1)S(1)} %get-tuple-element.58), channel_id=1, source_target_pairs={{0,1},{1,0},{2,3},{3,2},{4,5},{5,4},{6,7},{7,6},{8,9},{9,8},{10,11... | collective-permute-start | bytes 589832 | tf_op jit(solution)/shard_map/ppermute | solution.py:363
  3.6 2.6 %collective-permute-start.5 = (bf16[192,512]{1,0:T(8,128)(2,1)S(1)}, bf16[192,512]{1,0:T(8,128)(2,1)S(1)}, u32[]{:S(2)}, u32[]{:S(2)}) collective-permute-start(bf16[192,512]{1,0:T(8,128)(2,1)S(1)} %get-tuple-element.70), channel_id=1, source_target_pairs={{0,2},{1,4},{2,0},{3,6},{4,1},{5,8},{6,3},{7,10},{8,5},{9,12},{10,... | collective-permute-start | bytes 589832 | tf_op jit(solution)/shard_map/ppermute | solution.py:364
  6.4 2.0 %collective-permute-start.4 = (bf16[5,8,512]{2,1,0:T(8,128)(2,1)S(1)}, bf16[5,8,512]{2,1,0:T(8,128)(2,1)S(1)}, u32[]{:S(2)}, u32[]{:S(2)}) collective-permute-start(bf16[5,8,512]{2,1,0:T(8,128)(2,1)S(1)} %get-tuple-element.68), channel_id=1, source_target_pairs={{0,2},{1,3},{2,0},{3,1},{4,6},{5,7},{6,4},{7,5},{8,10},{9,11},{10,... | collective-permute-start | bytes 122888 | tf_op jit(solution)/shard_map/ppermute | solution.py:375
  8.5 2.4 %collective-permute-done.3.refs_9_ = bf16[5,8,512]{2,1,0:T(8,128)(2,1)S(1)} collective-permute-done((bf16[5,8,512]{2,1,0:T(8,128)(2,1)S(1)}, bf16[5,8,512]{2,1,0:T(8,128)(2,1)S(1)}, u32[]{:S(2)}, u32[]{:S(2)}) %collective-permute-start.3) | collective-permute-done | bytes 40992 | tf_op jit(solution)/shard_map/ppermute | solution.py:375
  10.9 0.6 %collective-permute-done.4.refs_11_ = bf16[5,8,512]{2,1,0:T(8,128)(2,1)S(1)} collective-permute-done((bf16[5,8,512]{2,1,0:T(8,128)(2,1)S(1)}, bf16[5,8,512]{2,1,0:T(8,128)(2,1)S(1)}, u32[]{:S(2)}, u32[]{:S(2)}) %collective-permute-start.4) | collective-permute-done | bytes 40992 | tf_op jit(solution)/shard_map/ppermute | solution.py:375
  11.5 1.3 %shard_map.90 = (f32[192,512]{1,0:T(8,128)S(1)}, f32[192,512]{1,0:T(8,128)S(1)}, bf16[192,512]{1,0:T(8,128)(2,1)S(1)}, f32[192,512]{1,0:T(8,128)S(1)}, f32[192,512]{1,0:T(8,128)S(1)}) custom-call(s32[8,128]{1,0:T(8,128)S(1)} %get-tuple-element.54.refs_0_, f32[192,512]{1,0:T(8,128)S(1)} %get-tuple-element.56.refs_1_, ...), custom_call_target="tpu_custom_call" | custom-call | tf_op jit(solution)/shard_map/pallas_call | solution.py:34
  13.3 2.1 %collective-permute-start.7 = (bf16[192,512]{1,0:T(8,128)(2,1)S(1)}, bf16[192,512]{1,0:T(8,128)(2,1)S(1)}, u32[]{:S(2)}, u32[]{:S(2)}) collective-permute-start(bf16[192,512]{1,0:T(8,128)(2,1)S(1)} %get-tuple-element.77), channel_id=1, source_target_pairs={{0,2},{1,4},{2,0},{3,6},{4,1},{5,8},{6,3},{7,10},{8,5},{9,12},{10,... | collective-permute-start | bytes 589832 | tf_op jit(solution)/shard_map/ppermute | solution.py:364
  15.4 1.2 %shard_map.92 = (f32[192,512]{1,0:T(8,128)S(1)}, f32[192,512]{1,0:T(8,128)S(1)}, bf16[192,512]{1,0:T(8,128)(2,1)S(1)}) custom-call(s32[8,128]{1,0:T(8,128)S(1)} %get-tuple-element.54.refs_0_, f32[192,512]{1,0:T(8,128)S(1)} %get-tuple-element.71.refs_1_.refs_7_, f32[192,512]{1,0:T(8,128)S(1)} %get-tuple-element.72.refs_2_, ...), custom_call_target="tpu_custom_call" | custom-call | tf_op jit(solution)/shard_map/pallas_call | solution.py:34
  16.8 2.2 %collective-permute-done.7.refs_2_ = bf16[192,512]{1,0:T(8,128)(2,1)S(1)} collective-permute-done((bf16[192,512]{1,0:T(8,128)(2,1)S(1)}, bf16[192,512]{1,0:T(8,128)(2,1)S(1)}, u32[]{:S(2)}, u32[]{:S(2)}) %collective-permute-start.7) | collective-permute-done | bytes 196640 | tf_op jit(solution)/shard_map/ppermute | solution.py:364
  19.4 2.1 %collective-permute-start.11 = (bf16[192,512]{1,0:T(8,128)(2,1)S(1)}, bf16[192,512]{1,0:T(8,128)(2,1)S(1)}, u32[]{:S(2)}, u32[]{:S(2)}) collective-permute-start(bf16[192,512]{1,0:T(8,128)(2,1)S(1)} %get-tuple-element.86), channel_id=1, source_target_pairs={{0,2},{1,4},{2,0},{3,6},{4,1},{5,8},{6,3},{7,10},{8,5},{9,12},{10,... | collective-permute-start | bytes 589832 | tf_op jit(solution)/shard_map/ppermute | solution.py:364
  21.7 2.0 %collective-permute-start.9 = (bf16[5,8,512]{2,1,0:T(8,128)(2,1)S(1)}, bf16[5,8,512]{2,1,0:T(8,128)(2,1)S(1)}, u32[]{:S(2)}, u32[]{:S(2)}) collective-permute-start(bf16[5,8,512]{2,1,0:T(8,128)(2,1)S(1)} %get-tuple-element.83), channel_id=1, source_target_pairs={{0,2},{1,3},{2,0},{3,1},{4,6},{5,7},{6,4},{7,5},{8,10},{9,11},{10,... | collective-permute-start | bytes 122888 | tf_op jit(solution)/shard_map/ppermute | solution.py:375
  23.7 2.3 %collective-permute-done.10.refs_11_ = bf16[5,8,512]{2,1,0:T(8,128)(2,1)S(1)} collective-permute-done((bf16[5,8,512]{2,1,0:T(8,128)(2,1)S(1)}, bf16[5,8,512]{2,1,0:T(8,128)(2,1)S(1)}, u32[]{:S(2)}, u32[]{:S(2)}) %collective-permute-start.10) | collective-permute-done | bytes 40992 | tf_op jit(solution)/shard_map/ppermute | solution.py:375
  26.0 0.9 %collective-permute-done.9.refs_9_ = bf16[5,8,512]{2,1,0:T(8,128)(2,1)S(1)} collective-permute-done((bf16[5,8,512]{2,1,0:T(8,128)(2,1)S(1)}, bf16[5,8,512]{2,1,0:T(8,128)(2,1)S(1)}, u32[]{:S(2)}, u32[]{:S(2)}) %collective-permute-start.9) | collective-permute-done | bytes 40992 | tf_op jit(solution)/shard_map/ppermute | solution.py:375
  26.9 1.5 %shard_map.96 = (f32[192,512]{1,0:T(8,128)S(1)}, f32[192,512]{1,0:T(8,128)S(1)}, bf16[192,512]{1,0:T(8,128)(2,1)S(1)}, f32[192,512]{1,0:T(8,128)S(1)}, f32[192,5...) custom-call(s32[8,128]{1,0:T(8,128)S(1)} %get-tuple-element.54.refs_0_, ...), custom_call_target="tpu_custom_call" | custom-call | tf_op jit(solution)/shard_map/pallas_call | solution.py:34
  28.9 2.1 %collective-permute-start.13 = (bf16[192,512]{1,0:T(8,128)(2,1)S(1)}, bf16[192,512]{1,0:T(8,128)(2,1)S(1)}, u32[]{:S(2)}, u32[]{:S(2)}) collective-permute-start(bf16[192,512]{1,0:T(8,128)(2,1)S(1)} %get-tuple-element.93), channel_id=1, source_target_pairs={{0,2},{1,4},{2,0},{3,6},{4,1},{5,8},{6,3},{7,10},{8,5},{9,12},{10,... | collective-permute-start | bytes 589832 | tf_op jit(solution)/shard_map/ppermute | solution.py:364
  31.0 1.2 %shard_map.98 = (f32[192,512]{1,0:T(8,128)S(1)}, f32[192,512]{1,0:T(8,128)S(1)}) custom-call(s32[8,128]{1,0:T(8,128)S(1)} %get-tuple-element.54.refs_0_, f32[192,512]{1,0:T(8,128)S(1)} %get-tuple-element.87.refs_1_.refs_7_, f32[192,512]{1,0:T(8,128)S(1)} %get-tuple-element.88.refs_2_, bf16[192,512]{1,0:T(8,128)(2,1)S(1)} %collective-permute-done.12.refs_3_, ...), custom_call_target="tpu_custom_call" | custom-call | tf_op jit(solution)/shard_map/pallas_call | solution.py:34
  32.3 2.3 %collective-permute-done.13.refs_2_ = bf16[192,512]{1,0:T(8,128)(2,1)S(1)} collective-permute-done((bf16[192,512]{1,0:T(8,128)(2,1)S(1)}, bf16[192,512]{1,0:T(8,128)(2,1)S(1)}, u32[]{:S(2)}, u32[]{:S(2)}) %collective-permute-start.13) | collective-permute-done | bytes 196640 | tf_op jit(solution)/shard_map/ppermute | solution.py:364
  35.7 2.0 %collective-permute-start.18 = (bf16[5,8,512]{2,1,0:T(8,128)(2,1)S(1)}, bf16[5,8,512]{2,1,0:T(8,128)(2,1)S(1)}, u32[]{:S(2)}, u32[]{:S(2)}) collective-permute-start(bf16[5,8,512]{2,1,0:T(8,128)(2,1)S(1)} %get-tuple-element.95.refs_4_), channel_id=1, source_target_pairs={{0,2},{1,3},{2,0},{3,1},{4,6},{5,7},{6,4},{7,5},{8,10},{9,11},{10,... | collective-permute-start | bytes 122888 | tf_op jit(solution)/shard_map/ppermute | solution.py:375
  37.7 2.0 %collective-permute-done.18.refs_5_ = bf16[5,8,512]{2,1,0:T(8,128)(2,1)S(1)} collective-permute-done((bf16[5,8,512]{2,1,0:T(8,128)(2,1)S(1)}, bf16[5,8,512]{2,1,0:T(8,128)(2,1)S(1)}, u32[]{:S(2)}, u32[]{:S(2)}) %collective-permute-start.18) | collective-permute-done | bytes 40992 | tf_op jit(solution)/shard_map/ppermute | solution.py:375
  39.7 2.0 %collective-permute-done.17.refs_3_ = bf16[5,8,512]{2,1,0:T(8,128)(2,1)S(1)} collective-permute-done((bf16[5,8,512]{2,1,0:T(8,128)(2,1)S(1)}, bf16[5,8,512]{2,1,0:T(8,128)(2,1)S(1)}, u32[]{:S(2)}, u32[]{:S(2)}) %collective-permute-start.17) | collective-permute-done | bytes 40992 | tf_op jit(solution)/shard_map/ppermute | solution.py:375
  41.7 1.0 %shard_map.102 = (f32[4,24,2048]{2,1,0:T(8,128)}, f32[4,24,2048]{2,1,0:T(8,128)S(1)}) custom-call(f32[4,24,2048]{2,1,0:T(8,128)S(1)} %copy-done.1, f32[192,512]{1,0:T(8,128)S(1)} %shard_map.100.refs_1_, f32[192,512]{1,0:T(8,128)S(1)} %get-tuple-element.94.refs_1_.refs_2_, f32[136,512]{1,0:T(8,128)S(1)} %collective-permute-done.14.refs_3_.refs_6_, ...), custom_call_target="tpu_custom_call" | custom-call | tf_op jit(solution)/shard_map/pallas_call | solution.py:34
  42.9 1.1 %shard_map.103 = f32[4,24,2048]{2,1,0:T(8,128)} custom-call(f32[4,24,2048]{2,1,0:T(8,128)S(1)} %get-tuple-element.102.refs_0_, f32[2,5,8,8,128]{4,3,2,1,0:T(8,128)S(1)} %get-tuple-element.63.refs_7_.refs_1_, f32[5,8,512]{2,1,0:T(8,128)S(1)} %get-tuple-element.103.refs_2_, bf16[5,8,512]{2,1,0:T(8,128)(2,1)S(1)} %collective-permute-done.17.refs_3_, ...), custom_call_target="tpu_custom_call" | custom-call | tf_op jit(solution)/shard_map/pallas_call | solution.py:34
  (40 shorter events, 3.6 us)
Async XLA Ops:
  0.6 2.3 %collective-permute-start = (bf16[4,24,2048]{2,1,0:T(8,128)(2,1)}, bf16[4,24,2048]{2,1,0:T(8,128)(2,1)S(1)}, u32[]{:S(2)}, u32[]{:S(2)}) collective-permute-start(bf16[4,24,2048]{2,1,0:T(8,128)(2,1)} %refs_3_.5), channel_id=1, source_target_pairs={{0,1},{1,0},{2,3},{3,2},{4,5},{5,4},{6,7},{7,6},{8,9},{9,8},{10,11... | collective-permute-start | bytes 1179656 | tf_op jit(solution)/shard_map/ppermute | solution.py:363
  2.8 8.7 %copy-start = (bf16[3,512,512]{2,1,0:T(8,128)(2,1)S(1)}, bf16[3,512,512]{2,1,0:T(8,128)(2,1)}, u32[]{:S(2)}) copy-start(bf16[3,512,512]{2,1,0:T(8,128)(2,1)} %refs_3_.9) | copy-start | bytes 4718596
  2.8 5.6 %collective-permute-start.2 = (f32[2,4,24,512]{3,2,1,0:T(8,128)S(1)}, f32[2,4,24,512]{3,2,1,0:T(8,128)S(1)}, u32[]{:S(2)}, u32[]{:S(2)}) collective-permute-start(f32[2,4,24,512]{3,2,1,0:T(8,128)S(1)} %get-tuple-element.60), channel_id=1, source_target_pairs={{0,1},{1,0},{2,3},{3,2},{4,5},{5,4},{6,7},{7,6},{8,9},{9,8},{10,11... | collective-permute-start | bytes 1179656 | tf_op jit(solution)/shard_map/ppermute | solution.py:363
  3.0 8.5 %collective-permute-start.1 = (bf16[192,512]{1,0:T(8,128)(2,1)S(1)}, bf16[192,512]{1,0:T(8,128)(2,1)S(1)}, u32[]{:S(2)}, u32[]{:S(2)}) collective-permute-start(bf16[192,512]{1,0:T(8,128)(2,1)S(1)} %get-tuple-element.58), channel_id=1, source_target_pairs={{0,1},{1,0},{2,3},{3,2},{4,5},{5,4},{6,7},{7,6},{8,9},{9,8},{10,11... | collective-permute-start | bytes 589832 | tf_op jit(solution)/shard_map/ppermute | solution.py:363
  3.6 9.4 %collective-permute-start.5 = (bf16[192,512]{1,0:T(8,128)(2,1)S(1)}, bf16[192,512]{1,0:T(8,128)(2,1)S(1)}, u32[]{:S(2)}, u32[]{:S(2)}) collective-permute-start(bf16[192,512]{1,0:T(8,128)(2,1)S(1)} %get-tuple-element.70), channel_id=1, source_target_pairs={{0,2},{1,4},{2,0},{3,6},{4,1},{5,8},{6,3},{7,10},{8,5},{9,12},{10,... | collective-permute-start | bytes 589832 | tf_op jit(solution)/shard_map/ppermute | solution.py:364
  6.3 4.6 %collective-permute-start.3 = (bf16[5,8,512]{2,1,0:T(8,128)(2,1)S(1)}, bf16[5,8,512]{2,1,0:T(8,128)(2,1)S(1)}, u32[]{:S(2)}, u32[]{:S(2)}) collective-permute-start(bf16[5,8,512]{2,1,0:T(8,128)(2,1)S(1)} %get-tuple-element.66), channel_id=1, source_target_pairs={{0,2},{1,3},{2,0},{3,1},{4,6},{5,7},{6,4},{7,5},{8,10},{9,11},{10,... | collective-permute-start | bytes 122888 | tf_op jit(solution)/shard_map/ppermute | solution.py:375
  6.4 5.1 %collective-permute-start.4 = (bf16[5,8,512]{2,1,0:T(8,128)(2,1)S(1)}, bf16[5,8,512]{2,1,0:T(8,128)(2,1)S(1)}, u32[]{:S(2)}, u32[]{:S(2)}) collective-permute-start(bf16[5,8,512]{2,1,0:T(8,128)(2,1)S(1)} %get-tuple-element.68), channel_id=1, source_target_pairs={{0,2},{1,3},{2,0},{3,1},{4,6},{5,7},{6,4},{7,5},{8,10},{9,11},{10,... | collective-permute-start | bytes 122888 | tf_op jit(solution)/shard_map/ppermute | solution.py:375
  12.8 2.6 %collective-permute-start.6 = (bf16[192,512]{1,0:T(8,128)(2,1)S(1)}, bf16[192,512]{1,0:T(8,128)(2,1)S(1)}, u32[]{:S(2)}, u32[]{:S(2)}) collective-permute-start(bf16[192,512]{1,0:T(8,128)(2,1)S(1)} %get-tuple-element.73), channel_id=1, source_target_pairs={{0,1},{1,0},{2,3},{3,2},{4,5},{5,4},{6,7},{7,6},{8,9},{9,8},{10,11... | collective-permute-start | bytes 589832 | tf_op jit(solution)/shard_map/ppermute | solution.py:363
  13.3 5.7 %collective-permute-start.7 = (bf16[192,512]{1,0:T(8,128)(2,1)S(1)}, bf16[192,512]{1,0:T(8,128)(2,1)S(1)}, u32[]{:S(2)}, u32[]{:S(2)}) collective-permute-start(bf16[192,512]{1,0:T(8,128)(2,1)S(1)} %get-tuple-element.77), channel_id=1, source_target_pairs={{0,2},{1,4},{2,0},{3,6},{4,1},{5,8},{6,3},{7,10},{8,5},{9,12},{10,... | collective-permute-start | bytes 589832 | tf_op jit(solution)/shard_map/ppermute | solution.py:364
  16.6 10.3 %collective-permute-start.8 = (bf16[192,512]{1,0:T(8,128)(2,1)S(1)}, bf16[192,512]{1,0:T(8,128)(2,1)S(1)}, u32[]{:S(2)}, u32[]{:S(2)}) collective-permute-start(bf16[192,512]{1,0:T(8,128)(2,1)S(1)} %get-tuple-element.81), channel_id=1, source_target_pairs={{0,1},{1,0},{2,3},{3,2},{4,5},{5,4},{6,7},{7,6},{8,9},{9,8},{10,11... | collective-permute-start | bytes 589832 | tf_op jit(solution)/shard_map/ppermute | solution.py:363
  19.4 9.0 %collective-permute-start.11 = (bf16[192,512]{1,0:T(8,128)(2,1)S(1)}, bf16[192,512]{1,0:T(8,128)(2,1)S(1)}, u32[]{:S(2)}, u32[]{:S(2)}) collective-permute-start(bf16[192,512]{1,0:T(8,128)(2,1)S(1)} %get-tuple-element.86), channel_id=1, source_target_pairs={{0,2},{1,4},{2,0},{3,6},{4,1},{5,8},{6,3},{7,10},{8,5},{9,12},{10,... | collective-permute-start | bytes 589832 | tf_op jit(solution)/shard_map/ppermute | solution.py:364
  21.5 4.5 %collective-permute-start.10 = (bf16[5,8,512]{2,1,0:T(8,128)(2,1)S(1)}, bf16[5,8,512]{2,1,0:T(8,128)(2,1)S(1)}, u32[]{:S(2)}, u32[]{:S(2)}) collective-permute-start(bf16[5,8,512]{2,1,0:T(8,128)(2,1)S(1)} %get-tuple-element.79.refs_4_), channel_id=1, source_target_pairs={{0,2},{1,3},{2,0},{3,1},{4,6},{5,7},{6,4},{7,5},{8,10},{9,11},{10,... | collective-permute-start | bytes 122888 | tf_op jit(solution)/shard_map/ppermute | solution.py:375
  21.7 5.2 %collective-permute-start.9 = (bf16[5,8,512]{2,1,0:T(8,128)(2,1)S(1)}, bf16[5,8,512]{2,1,0:T(8,128)(2,1)S(1)}, u32[]{:S(2)}, u32[]{:S(2)}) collective-permute-start(bf16[5,8,512]{2,1,0:T(8,128)(2,1)S(1)} %get-tuple-element.83), channel_id=1, source_target_pairs={{0,2},{1,3},{2,0},{3,1},{4,6},{5,7},{6,4},{7,5},{8,10},{9,11},{10,... | collective-permute-start | bytes 122888 | tf_op jit(solution)/shard_map/ppermute | solution.py:375
  28.4 2.6 %collective-permute-start.12 = (bf16[192,512]{1,0:T(8,128)(2,1)S(1)}, bf16[192,512]{1,0:T(8,128)(2,1)S(1)}, u32[]{:S(2)}, u32[]{:S(2)}) collective-permute-start(bf16[192,512]{1,0:T(8,128)(2,1)S(1)} %get-tuple-element.89), channel_id=1, source_target_pairs={{0,1},{1,0},{2,3},{3,2},{4,5},{5,4},{6,7},{7,6},{8,9},{9,8},{10,11... | collective-permute-start | bytes 589832 | tf_op jit(solution)/shard_map/ppermute | solution.py:363
  28.9 5.7 %collective-permute-start.13 = (bf16[192,512]{1,0:T(8,128)(2,1)S(1)}, bf16[192,512]{1,0:T(8,128)(2,1)S(1)}, u32[]{:S(2)}, u32[]{:S(2)}) collective-permute-start(bf16[192,512]{1,0:T(8,128)(2,1)S(1)} %get-tuple-element.93), channel_id=1, source_target_pairs={{0,2},{1,4},{2,0},{3,6},{4,1},{5,8},{6,3},{7,10},{8,5},{9,12},{10,... | collective-permute-start | bytes 589832 | tf_op jit(solution)/shard_map/ppermute | solution.py:364
  30.9 10.8 %collective-permute-start.16 = (f32[2,96,512]{2,1,0:T(8,128)S(1)}, f32[2,96,512]{2,1,0:T(8,128)S(1)}, u32[]{:S(2)}, u32[]{:S(2)}) collective-permute-start(f32[2,96,512]{2,1,0:T(8,128)S(1)} %get-tuple-element.100), channel_id=1, source_target_pairs={{0,1},{1,0},{2,3},{3,2},{4,5},{5,4},{6,7},{7,6},{8,9},{9,8},{10,11... | collective-permute-start | bytes 1179656 | tf_op jit(solution)/shard_map/ppermute | solution.py:363
  34.6 7.1 %copy-start.1 = (f32[4,24,2048]{2,1,0:T(8,128)S(1)}, f32[4,24,2048]{2,1,0:T(8,128)}, u32[]{:S(2)}) copy-start(f32[4,24,2048]{2,1,0:T(8,128)} %refs_0_.3) | copy-start | bytes 2359300
  35.1 6.6 %collective-permute-start.14 = (f32[136,512]{1,0:T(8,128)S(1)}, f32[136,512]{1,0:T(8,128)S(1)}, u32[]{:S(2)}, u32[]{:S(2)}) collective-permute-start(f32[136,512]{1,0:T(8,128)S(1)} %get-tuple-element.96), channel_id=1, source_target_pairs={{0,1},{1,0},{2,3},{3,2},{4,5},{5,4},{6,7},{7,6},{8,9},{9,8},{10,11... | collective-permute-start | bytes 835592 | tf_op jit(solution)/shard_map/ppermute | solution.py:363
  35.3 6.4 %collective-permute-start.15 = (f32[136,512]{1,0:T(8,128)S(1)}, f32[136,512]{1,0:T(8,128)S(1)}, u32[]{:S(2)}, u32[]{:S(2)}) collective-permute-start(f32[136,512]{1,0:T(8,128)S(1)} %get-tuple-element.97), channel_id=1, source_target_pairs={{0,1},{1,0},{2,3},{3,2},{4,5},{5,4},{6,7},{7,6},{8,9},{9,8},{10,11... | collective-permute-start | bytes 835592 | tf_op jit(solution)/shard_map/ppermute | solution.py:363
  35.7 4.0 %collective-permute-start.18 = (bf16[5,8,512]{2,1,0:T(8,128)(2,1)S(1)}, bf16[5,8,512]{2,1,0:T(8,128)(2,1)S(1)}, u32[]{:S(2)}, u32[]{:S(2)}) collective-permute-start(bf16[5,8,512]{2,1,0:T(8,128)(2,1)S(1)} %get-tuple-element.95.refs_4_), channel_id=1, source_target_pairs={{0,2},{1,3},{2,0},{3,1},{4,6},{5,7},{6,4},{7,5},{8,10},{9,11},{10,... | collective-permute-start | bytes 122888 | tf_op jit(solution)/shard_map/ppermute | solution.py:375
  37.7 4.0 %collective-permute-start.17 = (bf16[5,8,512]{2,1,0:T(8,128)(2,1)S(1)}, bf16[5,8,512]{2,1,0:T(8,128)(2,1)S(1)}, u32[]{:S(2)}, u32[]{:S(2)}) collective-permute-start(bf16[5,8,512]{2,1,0:T(8,128)(2,1)S(1)} %get-tuple-element.104), channel_id=1, source_target_pairs={{0,2},{1,3},{2,0},{3,1},{4,6},{5,7},{6,4},{7,5},{8,10},{9,11},{10,... | collective-permute-start | bytes 122888 | tf_op jit(solution)/shard_map/ppermute | solution.py:375
  39.7 3.1 %collective-permute-start.20 = (bf16[5,8,512]{2,1,0:T(8,128)(2,1)S(1)}, bf16[5,8,512]{2,1,0:T(8,128)(2,1)S(1)}, u32[]{:S(2)}, u32[]{:S(2)}) collective-permute-start(bf16[5,8,512]{2,1,0:T(8,128)(2,1)S(1)} %collective-permute-done.18.refs_5_), channel_id=1, source_target_pairs={{0,1},{1,0},{2,3},{3,2},{4,5},{5,4},{6,7},{7,6},{8,9},{9,8},{10,11... | collective-permute-start | bytes 122888 | tf_op jit(solution)/shard_map/ppermute | solution.py:363
  41.7 1.2 %collective-permute-start.19 = (bf16[5,8,512]{2,1,0:T(8,128)(2,1)S(1)}, bf16[5,8,512]{2,1,0:T(8,128)(2,1)S(1)}, u32[]{:S(2)}, u32[]{:S(2)}) collective-permute-start(bf16[5,8,512]{2,1,0:T(8,128)(2,1)S(1)} %collective-permute-done.17.refs_3_), channel_id=1, source_target_pairs={{0,1},{1,0},{2,3},{3,2},{4,5},{5,4},{6,7},{7,6},{8,9},{9,8},{10,11... | collective-permute-start | bytes 122888 | tf_op jit(solution)/shard_map/ppermute | solution.py:363

commit v3 on v2

v3 whole, which is shorter than its diff:
```python
import functools
import jax
import jax.numpy as jnp
from jax import lax
from jax.experimental import pallas as pl
from jax.experimental.pallas import tpu as pltpu
from jax.sharding import PartitionSpec as P

TILE = 512
SECTIONS = 4
NODES1 = 4
NODES2 = 16
ITERS = 2
PG_STEPS = 2
SUB = 8
AXES = ("space", "scen")
HALF = 0.5
VMEM_LIMIT = 8 << 20

f32, bf16 = jnp.float32, jnp.bfloat16
HBM = pl.BlockSpec(memory_space=pltpu.HBM)
VMEM = pl.BlockSpec(memory_space=pltpu.VMEM)
LANE = 128
SLOT_IN, SLOT_OUT, END, SLOT_EDGE, SLOT_OTHER = range(5)


def call(kernel, arrays, out, far=(), scratch=(), after=(), far_out=False):
    held = len(far) + len(arrays)

    def body(*refs):
        kernel(*refs[:held], *refs[held + len(after) :])

    return pl.pallas_call(
        body,
        out_shape=[jax.ShapeDtypeStruct(s, d) for s, d in out],
        in_specs=[HBM] * len(far) + [VMEM] * (len(arrays) + len(after)),
        out_specs=[HBM if far_out else VMEM] * len(out),
        scratch_shapes=list(scratch),
        compiler_params=pltpu.CompilerParams(vmem_limit_bytes=VMEM_LIMIT),
    )(*(pltpu.with_memory_space_constraint(x, pltpu.HBM) for x in far), *arrays, *after)


def lanes(tile):
    return pl.ds(pl.multiple_of(tile * TILE, TILE), TILE)


def rows_from(start, count):
    return pl.ds(pl.multiple_of(start, SUB), count)


class Plan:
    def __init__(self, mesh, fraction, cone_list, node_list):
        self.spaces, self.scens = mesh.shape["space"], mesh.shape["scen"]
        self.rank, self.periods, self.width = fraction.shape
        self.tiles = cone_list.shape[0]
        self.quarter = self.periods // SECTIONS
        self.local = 2 * self.rank
        self.total = node_list.shape[1]
        self.second = self.total > NODES2
        self.blocks = 1 + NODES1 + (NODES2 if self.second else 0)
        self.reach = (3 if self.second else 2) * self.quarter
        self.groups = -(-self.reach // SUB)
        self.top = self.groups * SUB
        self.parts = [(0, self.periods)]
        self.rows = self.local * self.periods
        self.own = self.rank * self.periods

    def part_of(self, low):
        return [low >= lo and low < hi for lo, hi in self.parts].index(True)

    def row(self, j, low, scenarios):
        lo, hi = self.parts[self.part_of(low)]
        return scenarios * lo + j * (hi - lo) + low - lo

    def section_of(self, block):
        return 0 if block == 0 else 1 if block <= NODES1 else 2

    def meets(self, low, section):
        return low < (section + 1) * self.quarter and low + SUB > section * self.quarter

    def blocks_at(self, low):
        return [b for b in range(self.blocks) if self.meets(low, self.section_of(b))]

    def core(self):
        return lax.axis_index("scen") % 2

    def edge_of(self, core):
        return core * (self.tiles - 1)

    def inner_of(self, core):
        return 1 + core * (self.tiles - 3)


class Rows:
    def __init__(self, plan, *refs):
        self.plan, self.refs = plan, refs

    def place(self, j, low):
        row = self.plan.row(j, low, self.plan.local)
        if len(self.refs) == 1:
            return self.refs[0], row
        part = self.plan.part_of(low)
        return self.refs[part], row - self.plan.local * self.plan.parts[part][0]

    def read(self, j, low, span):
        ref, row = self.place(j, low)
        return ref[rows_from(row, SUB), span]

    def all(self):
        return self.refs[0][...] if len(self.refs) == 1 else jnp.concatenate([ref[...] for ref in self.refs], axis=0)


def other_rows(plan, rows, out, parts=None):
    other = (1 - plan.core()) * plan.rank
    for part in range(len(plan.parts)) if parts is None else parts:
        lo, hi = plan.parts[part]
        count = plan.rank * (hi - lo)
        ref, row = rows.place(other, lo)
        at = plan.rank * lo if parts is None else 0
        out[at : at + count, :] = ref[rows_from(row, count), :]


def prepare_kernel(plan, *refs):
    small_far, (start, ore, dual) = refs[:3], refs[3:6]
    held, drive, drive_sent, control, share, select = refs[6:12]
    ores, duals, *small, sems = refs[12:]
    core = plan.core()
    copies = []
    for source, target in zip(small_far, small):
        copies.append(pltpu.make_async_copy(source, target, sems.at[len(copies)]))
    for k in range(2):
        for which, at in enumerate((core, 1 - core)):
            tile = (plan.edge_of, plan.inner_of)[k](at)
            fetch = [(ore, ores.at[which, k]), (dual, duals.at[which, k])] + ([(start, held.at[k])] if which == 0 else [])
            for source, target in fetch:
                copies.append(pltpu.make_async_copy(source.at[:, :, lanes(tile)], target, sems.at[len(copies)]))
    for copy in copies:
        copy.start()
    for copy in copies[: len(small)]:
        copy.wait()
    cones, nodes, chances = small
    edge, inner = plan.edge_of(core), plan.inner_of(core)
    base = lax.axis_index("space") * plan.tiles
    slot_in = jnp.where(cones[edge, 1] == base + inner, 1, 2)
    slot_out = 3 - slot_in
    end = jnp.where(cones[edge, slot_out] == base + edge, 1, 0)
    slot_edge = jnp.where(cones[inner, 1] == base + edge, 1, 2)
    place = lax.broadcasted_iota(jnp.int32, (SUB, LANE), 1)
    vector = jnp.zeros((SUB, LANE), jnp.int32)
    for k, v in enumerate((slot_in, slot_out, end, slot_edge, 3 - slot_edge)):
        vector = jnp.where(place == k, v, vector)
    control[...] = vector
    first = (lax.axis_index("scen") // 2) * plan.local
    splat = lambda v: jnp.full((SUB, LANE), v, f32)
    within = []
    for block in range(plan.blocks):
        section = plan.section_of(block)
        node = block - (1 if section == 1 else 1 + NODES1)
        total = jnp.float32(0)
        for other in range(plan.total):
            chance = chances[other]
            total = total + (jnp.where(nodes[section - 1, other] == node, chance, 0.0) if section else chance)
        within.append(1.0 / splat(total))
    for group in range(plan.groups):
        period = group * SUB + lax.broadcasted_iota(jnp.int32, (SUB, LANE), 0)
        for block in plan.blocks_at(group * SUB):
            section = plan.section_of(block)
            node = block - (1 if section == 1 else 1 + NODES1)
            inside = (period >= section * plan.quarter) & (period < (section + 1) * plan.quarter)
            mask = jnp.where(inside, 1.0, 0.0)
            for j in range(plan.local):
                chosen = mask
                if section:
                    chosen = mask * jnp.where(nodes[section - 1, first + j] == node, 1.0, 0.0)
                select[group, block, j] = chosen
                share[group, block, j] = chosen * (within[block] * chances[first + j])
    for copy in copies[len(small) :]:
        copy.wait()
    for k in range(2):
        drive[k] = ores[0, k].astype(f32) - duals[0, k]
        drive_sent[k] = ores[1, k].astype(f32) - duals[1, k]


def means_of_tile(plan, share, source, sums, sent):
    for chunk in range(TILE // LANE):
        span = slice(chunk * LANE, (chunk + 1) * LANE)
        totals = [jnp.zeros((SUB, LANE), f32)] * plan.blocks
        for low in range(0, plan.top, SUB):
            for j in range(plan.local):
                value = source.read(j, low, span) - HALF
                for block in plan.blocks_at(low):
                    totals[block] = totals[block] + share[low // SUB, block, j] * value
        for block in range(plan.blocks):
            sums[block, :, span] = totals[block]
            if sent is not None:
                sent[block, :, span] = totals[block].astype(bf16)


def means_kernel(plan, short, final, share, *refs):
    count = (len(refs) - final) // (3 if short else 2)
    for k in range(count):
        means_of_tile(plan, share, Rows(plan, refs[k]), refs[count + k], refs[2 * count + k] if short else None)
    if final:
        source, sums, packed = refs[0], refs[1], refs[-1]
        other_rows(plan, Rows(plan, source), packed, None if source.shape[0] == plan.rows else [0])
        first = packed.shape[0] - plan.blocks * SUB
        for block in range(plan.blocks):
            packed[first + block * SUB : first + (block + 1) * SUB, :] = sums[block]


def whole_means(plan, pair, span):
    return [pair[0][b, :, span] + pair[1][b, :, span].astype(f32) + HALF for b in range(plan.blocks)]


def center_rows(plan, low, j, select, means, value):
    mean = jnp.zeros_like(value)
    for block in plan.blocks_at(low):
        mean = mean + select[low // SUB, block, j] * means[block]
    if low + SUB > plan.reach:
        period = low + lax.broadcasted_iota(jnp.int32, value.shape, 0)
        mean = jnp.where(period < plan.reach, mean, value)
    return mean


def assemble(plan, own, theirs, out):
    core = plan.core()
    for k, rows in enumerate(out):
        for r in range(plan.rank):
            for lo, hi in plan.parts:
                for at, source in ((core, own), (1 - core, theirs)):
                    ref, row = rows.place(at * plan.rank + r, lo)
                    ref[rows_from(row, hi - lo), :] = source(k, r, lo, hi).astype(f32)


def start_kernel(plan, held, came, *outs):
    n = len(plan.parts)
    tiles = (plan.edge_of(plan.core()), plan.inner_of(plan.core()))
    state, sends = outs[: n + 1], outs[n + 1 :]
    out = (Rows(plan, *state[:n]), Rows(plan, state[n]))
    assemble(plan, lambda k, r, lo, hi: held[k, r, lo:hi, :], lambda k, r, lo, hi: came[r, lo:hi, lanes(tiles[k])], out)
    for ref, send in zip(state, sends):
        send[...] = ref[...].astype(bf16)


def drive_kernel(plan, held, came, drive_e, drive_n):
    take = lambda ref: lambda k, r, lo, hi: ref[k, r, lo:hi, :]
    assemble(plan, take(held), take(came), (Rows(plan, drive_e), Rows(plan, drive_n)))


def cones(control, edge, inner, halo, patterns):
    round_e, round_n = edge.all().astype(bf16), inner[...].astype(bf16)
    dot = functools.partial(jnp.dot, preferred_element_type=f32)
    cone_n = dot(round_n, patterns[0]) + dot(round_e, patterns[control[0, SLOT_EDGE]]) + dot(halo[...], patterns[control[0, SLOT_OTHER]])
    return dot(round_e, patterns[0]) + dot(round_n, patterns[control[0, SLOT_IN]]), cone_n


def own_outside(control, edge, patterns):
    return jnp.dot(edge.all().astype(bf16), patterns[control[0, SLOT_OUT]], preferred_element_type=f32)


def stepped(value, cone, pull):
    return value - 0.4 * ((value - cone) + value - pull)


def cone_kernel(plan, control, *refs):
    *edges, inner, halo, patterns, cone_e, cone_n = refs
    edge = Rows(plan, *edges)
    cone_e[...], cone_n[...] = cones(control, edge, inner, halo, patterns)

    @pl.when(control[0, END] == 1)
    def _():
        cone_e[...] += own_outside(control, edge, patterns)


def center_kernel(plan, last_round, *refs):
    n = len(plan.parts)
    edge, inner = Rows(plan, *refs[:n]), Rows(plan, refs[n])
    cone_e, cone_n, drive_e, drive_n, select = refs[n + 1 : n + 6]
    means_refs = (refs[n + 6 : n + 8], refs[n + 8 : n + 10])
    base_e, next_n, send_n, pull_e, pull_n, *moved = refs[n + 10 :]
    for side, (value, cone, drive, pull) in enumerate(((edge, cone_e, drive_e, pull_e), (inner, cone_n, drive_n, pull_n))):
        for chunk in range(TILE // LANE):
            span = slice(chunk * LANE, (chunk + 1) * LANE)
            means = whole_means(plan, means_refs[side], span)
            for j in range(plan.local):
                for low in range(0, plan.periods, SUB):
                    row = plan.row(j, low, plan.local)
                    rows = slice(row, row + SUB)
                    now = value.read(j, low, span)
                    mean = center_rows(plan, low, j, select, means, now) if low < plan.top else now
                    drawn = drive[rows, span] + mean
                    if last_round and low < plan.top:
                        gap = now - mean
                        moved[side][rows, span] = gap
                        drawn = drawn - gap
                    pull[rows, span] = drawn
                    after = stepped(now, cone[rows, span], drawn)
                    if side == 0:
                        base_e[rows, span] = after
                    else:
                        next_n[rows, span] = jnp.clip(after, 0.0, 1.0)
    send_n[...] = next_n[...].astype(bf16)
    if last_round:
        for side in range(2):
            other_rows(plan, Rows(plan, moved[side]), moved[2].at[side])


def inside_kernel(plan, final, control, *refs):
    n = len(plan.parts)
    edge = Rows(plan, *refs[:n])
    inner, halo, pull_e, pull_n, patterns, base_e, next_n, *send_n = refs[n:]
    cone_e, cone_n = cones(control, edge, inner, halo, patterns)
    value = jnp.clip(stepped(inner[...], cone_n, pull_n[...]), 0.0, 1.0)
    next_n[...] = value
    if not final:
        send_n[0][...] = value.astype(bf16)
    base_e[...] = stepped(edge.all(), cone_e, pull_e[...])

    @pl.when(control[0, END] == 1)
    def _():
        base_e[...] += 0.4 * own_outside(control, edge, patterns)


def outside_kernel(plan, part, control, base, halo, patterns, next_e, *send_e):
    lo, hi = plan.parts[part]
    scale = 0.4 * (1 - control[0, END]).astype(f32)
    cone = jnp.dot(halo[...], patterns[control[0, SLOT_OUT]], preferred_element_type=f32)
    value = jnp.clip(base[plan.local * lo : plan.local * hi, :] + scale * cone, 0.0, 1.0)
    next_e[...] = value
    if send_e:
        send_e[0][...] = value.astype(bf16)


def pick_kernel(plan, source, out):
    lo, hi = plan.parts[1]
    count = plan.rank * (hi - lo)
    out[...] = source[rows_from((1 - plan.core()) * count, count), :]


def own_tiles(plan, side, core):
    return (plan.edge_of, plan.inner_of)[side](core)


def fraction_kernel(plan, *refs):
    n = len(plan.parts)
    held = (Rows(plan, *refs[:n]), Rows(plan, refs[n]))
    packed_n, *packed_e, out = refs[n + 1 :]
    core = plan.core()
    for side in range(2):
        for r in range(plan.rank):
            for part, (lo, hi) in enumerate(plan.parts):
                ref, row = held[side].place(core * plan.rank + r, lo)
                out[r, lo:hi, lanes(own_tiles(plan, side, core))] = ref[rows_from(row, hi - lo), :]
                row = plan.row(r, lo, plan.rank)
                source = packed_n
                if side == 0:
                    source, row = packed_e[part], row - plan.rank * lo
                out[r, lo:hi, lanes(own_tiles(plan, side, 1 - core))] = source[row : row + hi - lo, :]


def price_kernel(plan, dual, edge, inner, packed_e, packed_n, moved_e, moved_n, moved_came, out):
    core = plan.core()
    count = plan.parts[0][1]
    period = lax.broadcasted_iota(jnp.int32, (plan.top, TILE), 0)
    for side, (value, packed, moved) in enumerate(((edge, packed_e, moved_e), (inner, packed_n, moved_n))):
        for r in range(plan.rank):
            own = rows_from((core * plan.rank + r) * count, plan.top)
            came = slice(r * count, r * count + plan.top)
            for at, now, gap in ((core, value[own, :], moved[own, :]), (1 - core, packed[came, :], moved_came[side, came, :])):
                where = lanes(own_tiles(plan, side, at))
                first = dual[r, : plan.top, where]
                out[r, :, where] = jnp.where(period < plan.reach, first + gap + now, first)


def finish_kernel(plan, offsets, dual, price, select, *refs):
    pairs = [[(refs[4 * p + 2 * s], refs[4 * p + 2 * s + 1]) for s in range(2)] for p in range(2)]
    out, made, sems = refs[-3:]
    core = plan.core()
    copies = []
    if plan.top < plan.periods:
        copies.append(pltpu.make_async_copy(dual.at[:, plan.top :, :], out.at[:, plan.top :, :], sems.at[plan.rank]))
        copies[0].start()
    for r in range(plan.rank):
        for owner in range(2):
            for side in range(2):
                tile = own_tiles(plan, side, core if owner == 0 else 1 - core)
                for chunk in range(TILE // LANE):
                    span = slice(chunk * LANE, (chunk + 1) * LANE)
                    first, second = pairs[owner][side]
                    if owner and offsets[side]:
                        first = [first[offsets[side] + b * SUB : offsets[side] + (b + 1) * SUB, span] for b in range(plan.blocks)]
                        means = [first[b] + second[b, :, span].astype(f32) + HALF for b in range(plan.blocks)]
                    else:
                        means = whole_means(plan, (first, second), span)
                    where = pl.ds(pl.multiple_of(tile * TILE + chunk * LANE, LANE), LANE)
                    for low in range(0, plan.top, SUB):
                        value = price[r, low : low + SUB, where]
                        for block in plan.blocks_at(low):
                            value = value - select[low // SUB, block, core * plan.rank + r] * means[block]
                        made[r, low : low + SUB, where] = value
        copy = pltpu.make_async_copy(made.at[r], out.at[r, : plan.top, :], sems.at[r])
        copy.start()
        copies.append(copy)
    for copy in copies:
        copy.wait()


def partners(plan):
    pairs = []
    for i in range(plan.spaces):
        for s in range(plan.scens):
            to = i + 1 if s % 2 else i - 1
            if 0 <= to < plan.spaces:
                pairs.append((i * plan.scens + s, to * plan.scens + (s ^ 1)))
            else:
                pairs.append((i * plan.scens + s, i * plan.scens + (s ^ 2 if plan.scens % 4 == 0 else s)))
    return pairs


def tiled(plan, start, ore, dual, patterns, cone_list, node_list, probability):
    flip = [(i, i ^ 1) for i in range(plan.scens)]
    edges = partners(plan)

    swap = lambda x: lax.ppermute(x, "scen", flip)
    outer = lambda x: lax.ppermute(x, AXES, edges)
    jump = lambda x, bit: lax.ppermute(x, "scen", [(i, i ^ bit) for i in range(plan.scens)])
    part = lambda f, *a: functools.partial(f, plan, *a)
    half = (2, plan.rank, plan.periods, TILE)
    sums = (plan.blocks, SUB, TILE)
    shares = (plan.groups, plan.blocks, plan.local, SUB, LANE)
    whole = (plan.rows, TILE)
    halves = [(plan.local * (hi - lo), TILE) for lo, hi in plan.parts]
    ranks = range(len(plan.parts))
    bits = [1 << b for b in range(1, plan.scens.bit_length() - 1)]

    def across(x, sent):
        other = None
        for k, bit in enumerate(bits):
            if k:
                x = x + other.astype(f32)
                sent = x.astype(sent.dtype)
            other = jump(sent, bit)
        return x, (jnp.zeros_like(sent) if other is None else other), sent

    packed = [None, None]

    def means_of(sides, short=True, final=False):
        count = len(sides)
        arrays = [(edge[0], inner)[k] for k in sides]
        outs = [(sums, f32)] * count + ([(sums, bf16)] * count if short else [])
        if final:
            outs += [((arrays[0].shape[0] // 2 + plan.blocks * SUB, TILE), f32)]
        got = call(part(means_kernel, short, final), [share, *arrays], outs)
        if final:
            packed[sides[0]] = swap(got[-1])
        return [across(got[k], got[count + k] if short else got[k]) for k in range(count)]

    came = swap(start)
    parts = (2, 2, plan.rank, plan.periods, TILE)
    held, drive_held, drive_sent, control, share, select = call(
        part(prepare_kernel), [],
        [(half, bf16), (half, f32), (half, f32), ((SUB, LANE), jnp.int32), (shares, f32), (shares, f32)],
        far=[cone_list, node_list, probability, start, ore, dual],
        scratch=[
            pltpu.VMEM(parts, bf16),
            pltpu.VMEM(parts, f32),
            *(pltpu.SMEM(x.shape, x.dtype) for x in (cone_list, node_list, probability)),
            pltpu.SemaphoreType.DMA((13,)),
        ],
    )
    n = len(ranks)
    shapes = [*halves, whole]
    got = call(part(start_kernel), [held, came], [(x, f32) for x in shapes] + [(x, bf16) for x in shapes])
    edge, inner = list(got[:n]), got[n]
    halo = [outer(got[n + 1 + c]) for c in ranks]
    halo_n = swap(got[2 * n + 1])
    means = means_of((0, 1))
    drive_came = swap(drive_sent)
    drive = call(part(drive_kernel), [drive_held, drive_came], [(whole, f32)] * 2)
    last = []
    for step in range(ITERS * PG_STEPS):
        closing = step % PG_STEPS == PG_STEPS - 1
        final = step == ITERS * PG_STEPS - 1
        last_round = step >= PG_STEPS
        outs = [(whole, f32), (whole, f32)] + ([] if final else [(whole, bf16)])
        if step % PG_STEPS == 0:
            cone = call(part(cone_kernel), [control, *edge, inner, halo_n, patterns], [(whole, f32)] * 2, after=last)
            arrays = [*edge, inner, *cone, *drive, select, *means[0][:2], *means[1][:2]]
            outs += [(whole, f32)] * 2
            outs += [(whole, f32)] * 2 + [((2, plan.own, TILE), f32)] if last_round else []
            got = call(part(center_kernel, last_round), arrays, outs)
            pull = got[3:5]
            if last_round:
                moved = [*got[5:7], swap(got[7])]
        else:
            arrays = [control, *edge, inner, halo_n, *pull, patterns]
            got = call(part(inside_kernel, final), arrays, outs, after=last)
        base, inner = got[:2]
        last = [base]
        if not final:
            halo_n = swap(got[2])
        if closing:
            means_n = means_of((1,), short=final, final=final)
            last = [means_n[0][2]]
        for c in ranks:
            outs = [(halves[c], f32)] + ([] if final else [(halves[c], bf16)])
            got = call(part(outside_kernel, c), [control, base, halo[c], patterns], outs, after=last)
            edge[c] = got[0]
            last = [got[0]]
            if not final:
                halo[c] = outer(got[1])
            if closing and c == 0:
                means = means_of((0,), final=final) + means_n
                last = [means[0][2]]
    packed_rest = [swap(call(part(pick_kernel), [edge[1]], [((plan.rank * (plan.periods - plan.top), TILE), f32)])[0])] if n > 1 else []
    (fraction,) = call(part(fraction_kernel), [*edge, inner, packed[1], packed[0], *packed_rest], [(start.shape, f32)])
    prices = (plan.rank, plan.top, plan.width)
    (price,) = call(part(price_kernel), [dual, edge[0], inner, *packed, *moved], [(prices, f32)])
    if len(bits) == 1:
        theirs = [(packed[k], jump(means[k][2], 3)) for k in range(2)]
        offsets = tuple(x.shape[0] - plan.blocks * SUB for x in packed)
    else:
        theirs = [(swap(means[k][0]), swap(means[k][1])) for k in range(2)]
        offsets = (0, 0)
    arrays = [price, select, *means[0][:2], *means[1][:2], *theirs[0], *theirs[1]]
    (dual_out,) = call(
        part(finish_kernel, offsets), [dual, *arrays], [(start.shape, f32)], far_out=True,
        scratch=[pltpu.VMEM(prices, f32), pltpu.SemaphoreType.DMA((plan.rank + 1,))],
    )
    return fraction, dual_out


def solution(mesh):
    def body(start, ore, dual, patterns, cone_list, node_list, probability):
        plan = Plan(mesh, start, cone_list, node_list)
        assert plan.tiles == 4 and plan.scens % 2 == 0 and plan.periods % SUB == 0
        return tiled(plan, start, ore, dual, patterns, cone_list, node_list, probability)

    split = P("scen", None, "space")
    in_specs = (split, split, split, P(), P("space", None), P(), P())
    return jax.shard_map(body, mesh=mesh, in_specs=in_specs, out_specs=(split, split), check_vma=False)
```

time: 44.2 us -> 43.4 us (0.982)
  waiting for transfers between devices: 14.9 us -> 11.9 us
  starting transfers between devices: 17 us -> 18.8 us
    ppermute x6 -> x8, waiting for transfers between devices: 10.2 us -> 7.35 us  [tiled(): lax.ppermute(x, 'scen', [(i, i ^ bit) for i in range(plan.scens)])]
    ppermute x6 -> x8, starting transfers between devices: 6.23 us -> 8.02 us  [tiled(): lax.ppermute(x, 'scen', [(i, i ^ bit) for i in range(plan.scens)])]
    pallas_call x18 -> x21, Pallas kernels: 11.3 us -> 11.6 us  [call(): pl.pallas_call(body, out_shape=[jax.ShapeDtypeStruct(s, d) for s, d in ou...]
    ppermute x11 -> x9, starting transfers between devices: 1.99 us -> 1.99 us  [tiled(): swap = lambda x: lax.ppermute(x, 'scen', flip)]
  transfers between devices with their start and end apart: 21 -> 21, of which waited for: 9 -> 7; matrix products, arithmetic and copies ran while one was open for 0% -> 0% of each run, Pallas kernels for 23% -> 25%
where the time goes in v3:
time: 43.4 us; the launch traced here: 43.2 us
  starting transfers between devices  18.8 us (43%)
  waiting for transfers between devices  11.9 us (27%)
  Pallas kernels  11.6 us (27%)
  between operations  0.84 us (2%)
    pallas_call x21, Pallas kernels, call(): pl.pallas_call(body, out_shape=[jax.ShapeDtypeStruct(s, d) for s, d in ou...  11.6 us
    ppermute x4, starting transfers between devices, tiled(): outer = lambda x: lax.ppermute(x, AXES, edges)  8.81 us
    ppermute x8, starting transfers between devices, tiled(): lax.ppermute(x, 'scen', [(i, i ^ bit) for i in range(plan.scens)])  8.02 us
    ppermute x8, waiting for transfers between devices, tiled(): lax.ppermute(x, 'scen', [(i, i ^ bit) for i in range(plan.scens)])  7.35 us
    ppermute x4, waiting for transfers between devices, tiled(): outer = lambda x: lax.ppermute(x, AXES, edges)  4.55 us
    ppermute x9, starting transfers between devices, tiled(): swap = lambda x: lax.ppermute(x, 'scen', flip)  1.99 us
  transfers between devices with their start and end apart: 21, of which 7 were waited for; matrix products, arithmetic and copies ran while one was open for 0% of the time, Pallas kernels for 25%

profile of v3, /device:TPU:0, one launch (start us, length us, event | category | flops | bytes accessed | tf_op | source)
XLA Modules:
  0.0 43.2 jit_solution(16869090976125896867)
XLA Ops:
  0.6 0.6 %collective-permute-start = (bf16[4,24,2048]{2,1,0:T(8,128)(2,1)}, bf16[4,24,2048]{2,1,0:T(8,128)(2,1)S(1)}, u32[]{:S(2)}, u32[]{:S(2)}) collective-permute-start(bf16[4,24,2048]{2,1,0:T(8,128)(2,1)} %refs_3_.5), channel_id=1, source_target_pairs={{0,1},{1,0},{2,3},{3,2},{4,5},{5,4},{6,7},{7,6},{8,9},{9,8},{10,11... | collective-permute-start | bytes 1179656 | tf_op jit(solution)/shard_map/ppermute | solution.py:424
  1.2 1.6 %shard_map.86 = (bf16[2,4,24,512]{3,2,1,0:T(8,128)(2,1)S(1)}, f32[2,4,24,512]{3,2,1,0:T(8,128)S(1)}, f32[2,4,24,512]{3,2,1,0:T(8,128)S(1)}, s32[8,128]{1,0:T(8,1...) custom-call(s32[4,3]{1,0:T(4,128)} %refs_0_.3, s32[2,16]{1,0:T(2,128)} %refs_1_.1, ...), custom_call_target="tpu_custom_call" | custom-call | tf_op jit(solution)/shard_map/pallas_call | solution.py:33
  3.0 0.5 %collective-permute-start.1 = (bf16[192,512]{1,0:T(8,128)(2,1)S(1)}, bf16[192,512]{1,0:T(8,128)(2,1)S(1)}, u32[]{:S(2)}, u32[]{:S(2)}) collective-permute-start(bf16[192,512]{1,0:T(8,128)(2,1)S(1)} %get-tuple-element.58), channel_id=1, source_target_pairs={{0,1},{1,0},{2,3},{3,2},{4,5},{5,4},{6,7},{7,6},{8,9},{9,8},{10,11... | collective-permute-start | bytes 589832 | tf_op jit(solution)/shard_map/ppermute | solution.py:424
  3.6 2.6 %collective-permute-start.5 = (bf16[192,512]{1,0:T(8,128)(2,1)S(1)}, bf16[192,512]{1,0:T(8,128)(2,1)S(1)}, u32[]{:S(2)}, u32[]{:S(2)}) collective-permute-start(bf16[192,512]{1,0:T(8,128)(2,1)S(1)} %get-tuple-element.72), channel_id=1, source_target_pairs={{0,2},{1,4},{2,0},{3,6},{4,1},{5,8},{6,3},{7,10},{8,5},{9,12},{10,... | collective-permute-start | bytes 589832 | tf_op jit(solution)/shard_map/ppermute | solution.py:425
  6.4 2.0 %collective-permute-start.4 = (bf16[5,8,512]{2,1,0:T(8,128)(2,1)S(1)}, bf16[5,8,512]{2,1,0:T(8,128)(2,1)S(1)}, u32[]{:S(2)}, u32[]{:S(2)}) collective-permute-start(bf16[5,8,512]{2,1,0:T(8,128)(2,1)S(1)} %get-tuple-element.70), channel_id=1, source_target_pairs={{0,2},{1,3},{2,0},{3,1},{4,6},{5,7},{6,4},{7,5},{8,10},{9,11},{10,... | collective-permute-start | bytes 122888 | tf_op jit(solution)/shard_map/ppermute | solution.py:426
  8.5 1.1 %shard_map.88 = (f32[192,512]{1,0:T(8,128)S(1)}, f32[192,512]{1,0:T(8,128)S(1)}) custom-call(s32[8,128]{1,0:T(8,128)S(1)} %get-tuple-element.54.refs_0_, f32[192,512]{1,0:T(8,128)S(1)} %get-tuple-element.56.refs_1_.refs_0_, f32[192,512]{1,0:T(8,128)S(1)} %get-tuple-element.57.refs_2_.refs_1_, bf16[192,512]{1,0:T(8,128)(2,1)S(1)} %collective-permute-done.1.refs_3_, ...), custom_call_target="tpu_custom_call" | custom-call | tf_op jit(solution)/shard_map/pallas_call | solution.py:33
  9.7 1.2 %collective-permute-done.3.refs_8_ = bf16[5,8,512]{2,1,0:T(8,128)(2,1)S(1)} collective-permute-done((bf16[5,8,512]{2,1,0:T(8,128)(2,1)S(1)}, bf16[5,8,512]{2,1,0:T(8,128)(2,1)S(1)}, u32[]{:S(2)}, u32[]{:S(2)}) %collective-permute-start.3) | collective-permute-done | bytes 40992 | tf_op jit(solution)/shard_map/ppermute | solution.py:426
  10.9 0.6 %collective-permute-done.4.refs_10_ = bf16[5,8,512]{2,1,0:T(8,128)(2,1)S(1)} collective-permute-done((bf16[5,8,512]{2,1,0:T(8,128)(2,1)S(1)}, bf16[5,8,512]{2,1,0:T(8,128)(2,1)S(1)}, u32[]{:S(2)}, u32[]{:S(2)}) %collective-permute-start.4) | collective-permute-done | bytes 40992 | tf_op jit(solution)/shard_map/ppermute | solution.py:426
  12.4 2.1 %collective-permute-start.7 = (bf16[192,512]{1,0:T(8,128)(2,1)S(1)}, bf16[192,512]{1,0:T(8,128)(2,1)S(1)}, u32[]{:S(2)}, u32[]{:S(2)}) collective-permute-start(bf16[192,512]{1,0:T(8,128)(2,1)S(1)} %get-tuple-element.79), channel_id=1, source_target_pairs={{0,2},{1,4},{2,0},{3,6},{4,1},{5,8},{6,3},{7,10},{8,5},{9,12},{10,... | collective-permute-start | bytes 589832 | tf_op jit(solution)/shard_map/ppermute | solution.py:425
  14.5 1.2 %shard_map.93 = (f32[192,512]{1,0:T(8,128)S(1)}, f32[192,512]{1,0:T(8,128)S(1)}, bf16[192,512]{1,0:T(8,128)(2,1)S(1)}) custom-call(s32[8,128]{1,0:T(8,128)S(1)} %get-tuple-element.54.refs_0_, f32[192,512]{1,0:T(8,128)S(1)} %get-tuple-element.73.refs_1_.refs_7_, f32[192,512]{1,0:T(8,128)S(1)} %get-tuple-element.74.refs_2_, ...), custom_call_target="tpu_custom_call" | custom-call | tf_op jit(solution)/shard_map/pallas_call | solution.py:33
  16.0 2.2 %collective-permute-done.7.refs_2_ = bf16[192,512]{1,0:T(8,128)(2,1)S(1)} collective-permute-done((bf16[192,512]{1,0:T(8,128)(2,1)S(1)}, bf16[192,512]{1,0:T(8,128)(2,1)S(1)}, u32[]{:S(2)}, u32[]{:S(2)}) %collective-permute-start.7) | collective-permute-done | bytes 196640 | tf_op jit(solution)/shard_map/ppermute | solution.py:425
  18.6 2.1 %collective-permute-start.11 = (bf16[192,512]{1,0:T(8,128)(2,1)S(1)}, bf16[192,512]{1,0:T(8,128)(2,1)S(1)}, u32[]{:S(2)}, u32[]{:S(2)}) collective-permute-start(bf16[192,512]{1,0:T(8,128)(2,1)S(1)} %get-tuple-element.88), channel_id=1, source_target_pairs={{0,2},{1,4},{2,0},{3,6},{4,1},{5,8},{6,3},{7,10},{8,5},{9,12},{10,... | collective-permute-start | bytes 589832 | tf_op jit(solution)/shard_map/ppermute | solution.py:425
  20.9 2.0 %collective-permute-start.9 = (bf16[5,8,512]{2,1,0:T(8,128)(2,1)S(1)}, bf16[5,8,512]{2,1,0:T(8,128)(2,1)S(1)}, u32[]{:S(2)}, u32[]{:S(2)}) collective-permute-start(bf16[5,8,512]{2,1,0:T(8,128)(2,1)S(1)} %get-tuple-element.83.refs_5_), channel_id=1, source_target_pairs={{0,2},{1,3},{2,0},{3,1},{4,6},{5,7},{6,4},{7,5},{8,10},{9,11},{10,... | collective-permute-start | bytes 122888 | tf_op jit(solution)/shard_map/ppermute | solution.py:426
  22.9 1.1 %shard_map.97 = (f32[192,512]{1,0:T(8,128)S(1)}, f32[192,512]{1,0:T(8,128)S(1)}) custom-call(s32[8,128]{1,0:T(8,128)S(1)} %get-tuple-element.54.refs_0_, f32[192,512]{1,0:T(8,128)S(1)} %get-tuple-element.81.refs_1_.refs_0_, f32[192,512]{1,0:T(8,128)S(1)} %get-tuple-element.80.refs_1_.refs_2_, bf16[192,512]{1,0:T(8,128)(2,1)S(1)} %collective-permute-done.8.refs_3_, ...), custom_call_target="tpu_custom_call" | custom-call | tf_op jit(solution)/shard_map/pallas_call | solution.py:33
  24.0 2.9 %collective-permute-done.9.refs_8_ = bf16[5,8,512]{2,1,0:T(8,128)(2,1)S(1)} collective-permute-done((bf16[5,8,512]{2,1,0:T(8,128)(2,1)S(1)}, bf16[5,8,512]{2,1,0:T(8,128)(2,1)S(1)}, u32[]{:S(2)}, u32[]{:S(2)}) %collective-permute-start.9) | collective-permute-done | bytes 40992 | tf_op jit(solution)/shard_map/ppermute | solution.py:426
  27.9 2.1 %collective-permute-start.13 = (bf16[192,512]{1,0:T(8,128)(2,1)S(1)}, bf16[192,512]{1,0:T(8,128)(2,1)S(1)}, u32[]{:S(2)}, u32[]{:S(2)}) collective-permute-start(bf16[192,512]{1,0:T(8,128)(2,1)S(1)} %get-tuple-element.95), channel_id=1, source_target_pairs={{0,2},{1,4},{2,0},{3,6},{4,1},{5,8},{6,3},{7,10},{8,5},{9,12},{10,... | collective-permute-start | bytes 589832 | tf_op jit(solution)/shard_map/ppermute | solution.py:425
  30.0 1.2 %shard_map.100 = (f32[192,512]{1,0:T(8,128)S(1)}, f32[192,512]{1,0:T(8,128)S(1)}) custom-call(s32[8,128]{1,0:T(8,128)S(1)} %get-tuple-element.54.refs_0_, f32[192,512]{1,0:T(8,128)S(1)} %get-tuple-element.89.refs_1_.refs_7_, f32[192,512]{1,0:T(8,128)S(1)} %get-tuple-element.90.refs_2_, bf16[192,512]{1,0:T(8,128)(2,1)S(1)} %collective-permute-done.12.refs_3_, ...), custom_call_target="tpu_custom_call" | custom-call | tf_op jit(solution)/shard_map/pallas_call | solution.py:33
  31.3 2.3 %collective-permute-done.13.refs_2_ = bf16[192,512]{1,0:T(8,128)(2,1)S(1)} collective-permute-done((bf16[192,512]{1,0:T(8,128)(2,1)S(1)}, bf16[192,512]{1,0:T(8,128)(2,1)S(1)}, u32[]{:S(2)}, u32[]{:S(2)}) %collective-permute-start.13) | collective-permute-done | bytes 196640 | tf_op jit(solution)/shard_map/ppermute | solution.py:425
  34.7 1.7 %collective-permute-start.20 = (bf16[5,8,512]{2,1,0:T(8,128)(2,1)S(1)}, bf16[5,8,512]{2,1,0:T(8,128)(2,1)S(1)}, u32[]{:S(2)}, u32[]{:S(2)}) collective-permute-start(bf16[5,8,512]{2,1,0:T(8,128)(2,1)S(1)} %get-tuple-element.97.refs_4_), channel_id=1, source_target_pairs={{0,3},{1,2},{2,1},{3,0},{4,7},{5,6},{6,5},{7,4},{8,11},{9,10},{10,... | collective-permute-start | bytes 122888 | tf_op jit(solution)/shard_map/ppermute | solution.py:426
  36.7 1.5 %collective-permute-start.19 = (bf16[5,8,512]{2,1,0:T(8,128)(2,1)S(1)}, bf16[5,8,512]{2,1,0:T(8,128)(2,1)S(1)}, u32[]{:S(2)}, u32[]{:S(2)}) collective-permute-start(bf16[5,8,512]{2,1,0:T(8,128)(2,1)S(1)} %get-tuple-element.104), channel_id=1, source_target_pairs={{0,3},{1,2},{2,1},{3,0},{4,7},{5,6},{6,5},{7,4},{8,11},{9,10},{10,... | collective-permute-start | bytes 122888 | tf_op jit(solution)/shard_map/ppermute | solution.py:426
  38.5 0.9 %shard_map.104 = f32[4,24,2048]{2,1,0:T(8,128)} custom-call(f32[192,512]{1,0:T(8,128)S(1)} %shard_map.102.refs_1_.refs_0_, f32[192,512]{1,0:T(8,128)S(1)} %get-tuple-element.96.refs_1_.refs_2_, f32[136,512]{1,0:T(8,128)S(1)} %collective-permute-done.14.refs_2_.refs_4_.refs_9_, f32[136,512]{1,0:T(8,128)S(1)} %collective-permute-done.15.refs_3_.refs_7_), custom_call_target="tpu_custom_call" | custom-call | tf_op jit(solution)/shard_map/pallas_call | solution.py:33
  39.6 1.1 %collective-permute-done.18.refs_6_ = bf16[5,8,512]{2,1,0:T(8,128)(2,1)S(1)} collective-permute-done((bf16[5,8,512]{2,1,0:T(8,128)(2,1)S(1)}, bf16[5,8,512]{2,1,0:T(8,128)(2,1)S(1)}, u32[]{:S(2)}, u32[]{:S(2)}) %collective-permute-start.18) | collective-permute-done | bytes 40992 | tf_op jit(solution)/shard_map/ppermute | solution.py:426
  40.7 1.4 %collective-permute-done.17.refs_4_ = bf16[5,8,512]{2,1,0:T(8,128)(2,1)S(1)} collective-permute-done((bf16[5,8,512]{2,1,0:T(8,128)(2,1)S(1)}, bf16[5,8,512]{2,1,0:T(8,128)(2,1)S(1)}, u32[]{:S(2)}, u32[]{:S(2)}) %collective-permute-start.17) | collective-permute-done | bytes 40992 | tf_op jit(solution)/shard_map/ppermute | solution.py:426
  42.2 1.0 %shard_map.106 = f32[4,24,2048]{2,1,0:T(8,128)} custom-call(f32[4,24,2048]{2,1,0:T(8,128)S(1)} %copy-done.1, f32[4,16,2048]{2,1,0:T(8,128)S(1)} %shard_map.105.refs_1_, f32[2,5,8,8,128]{4,3,2,1,0:T(8,128)S(1)} %get-tuple-element.65.refs_6_.refs_2_, f32[5,8,512]{2,1,0:T(8,128)S(1)} %get-tuple-element.103.refs_3_, ...), custom_call_target="tpu_custom_call" | custom-call | tf_op jit(solution)/shard_map/pallas_call | solution.py:33
  (43 shorter events, 5.1 us)
Async XLA Ops:
  0.6 2.3 %collective-permute-start = (bf16[4,24,2048]{2,1,0:T(8,128)(2,1)}, bf16[4,24,2048]{2,1,0:T(8,128)(2,1)S(1)}, u32[]{:S(2)}, u32[]{:S(2)}) collective-permute-start(bf16[4,24,2048]{2,1,0:T(8,128)(2,1)} %refs_3_.5), channel_id=1, source_target_pairs={{0,1},{1,0},{2,3},{3,2},{4,5},{5,4},{6,7},{7,6},{8,9},{9,8},{10,11... | collective-permute-start | bytes 1179656 | tf_op jit(solution)/shard_map/ppermute | solution.py:424
  2.8 5.7 %copy-start = (bf16[3,512,512]{2,1,0:T(8,128)(2,1)S(1)}, bf16[3,512,512]{2,1,0:T(8,128)(2,1)}, u32[]{:S(2)}) copy-start(bf16[3,512,512]{2,1,0:T(8,128)(2,1)} %refs_3_.9) | copy-start | bytes 4718596
  2.8 5.6 %collective-permute-start.2 = (f32[2,4,24,512]{3,2,1,0:T(8,128)S(1)}, f32[2,4,24,512]{3,2,1,0:T(8,128)S(1)}, u32[]{:S(2)}, u32[]{:S(2)}) collective-permute-start(f32[2,4,24,512]{3,2,1,0:T(8,128)S(1)} %get-tuple-element.62), channel_id=1, source_target_pairs={{0,1},{1,0},{2,3},{3,2},{4,5},{5,4},{6,7},{7,6},{8,9},{9,8},{10,11... | collective-permute-start | bytes 1179656 | tf_op jit(solution)/shard_map/ppermute | solution.py:424
  3.0 5.5 %collective-permute-start.1 = (bf16[192,512]{1,0:T(8,128)(2,1)S(1)}, bf16[192,512]{1,0:T(8,128)(2,1)S(1)}, u32[]{:S(2)}, u32[]{:S(2)}) collective-permute-start(bf16[192,512]{1,0:T(8,128)(2,1)S(1)} %get-tuple-element.58), channel_id=1, source_target_pairs={{0,1},{1,0},{2,3},{3,2},{4,5},{5,4},{6,7},{7,6},{8,9},{9,8},{10,11... | collective-permute-start | bytes 589832 | tf_op jit(solution)/shard_map/ppermute | solution.py:424
  3.6 8.5 %collective-permute-start.5 = (bf16[192,512]{1,0:T(8,128)(2,1)S(1)}, bf16[192,512]{1,0:T(8,128)(2,1)S(1)}, u32[]{:S(2)}, u32[]{:S(2)}) collective-permute-start(bf16[192,512]{1,0:T(8,128)(2,1)S(1)} %get-tuple-element.72), channel_id=1, source_target_pairs={{0,2},{1,4},{2,0},{3,6},{4,1},{5,8},{6,3},{7,10},{8,5},{9,12},{10,... | collective-permute-start | bytes 589832 | tf_op jit(solution)/shard_map/ppermute | solution.py:425
  6.4 4.6 %collective-permute-start.3 = (bf16[5,8,512]{2,1,0:T(8,128)(2,1)S(1)}, bf16[5,8,512]{2,1,0:T(8,128)(2,1)S(1)}, u32[]{:S(2)}, u32[]{:S(2)}) collective-permute-start(bf16[5,8,512]{2,1,0:T(8,128)(2,1)S(1)} %get-tuple-element.68), channel_id=1, source_target_pairs={{0,2},{1,3},{2,0},{3,1},{4,6},{5,7},{6,4},{7,5},{8,10},{9,11},{10,... | collective-permute-start | bytes 122888 | tf_op jit(solution)/shard_map/ppermute | solution.py:426
  6.4 5.1 %collective-permute-start.4 = (bf16[5,8,512]{2,1,0:T(8,128)(2,1)S(1)}, bf16[5,8,512]{2,1,0:T(8,128)(2,1)S(1)}, u32[]{:S(2)}, u32[]{:S(2)}) collective-permute-start(bf16[5,8,512]{2,1,0:T(8,128)(2,1)S(1)} %get-tuple-element.70), channel_id=1, source_target_pairs={{0,2},{1,3},{2,0},{3,1},{4,6},{5,7},{6,4},{7,5},{8,10},{9,11},{10,... | collective-permute-start | bytes 122888 | tf_op jit(solution)/shard_map/ppermute | solution.py:426
  12.0 2.6 %collective-permute-start.6 = (bf16[192,512]{1,0:T(8,128)(2,1)S(1)}, bf16[192,512]{1,0:T(8,128)(2,1)S(1)}, u32[]{:S(2)}, u32[]{:S(2)}) collective-permute-start(bf16[192,512]{1,0:T(8,128)(2,1)S(1)} %get-tuple-element.75), channel_id=1, source_target_pairs={{0,1},{1,0},{2,3},{3,2},{4,5},{5,4},{6,7},{7,6},{8,9},{9,8},{10,11... | collective-permute-start | bytes 589832 | tf_op jit(solution)/shard_map/ppermute | solution.py:424
  12.4 5.7 %collective-permute-start.7 = (bf16[192,512]{1,0:T(8,128)(2,1)S(1)}, bf16[192,512]{1,0:T(8,128)(2,1)S(1)}, u32[]{:S(2)}, u32[]{:S(2)}) collective-permute-start(bf16[192,512]{1,0:T(8,128)(2,1)S(1)} %get-tuple-element.79), channel_id=1, source_target_pairs={{0,2},{1,4},{2,0},{3,6},{4,1},{5,8},{6,3},{7,10},{8,5},{9,12},{10,... | collective-permute-start | bytes 589832 | tf_op jit(solution)/shard_map/ppermute | solution.py:425
  15.8 7.1 %collective-permute-start.8 = (bf16[192,512]{1,0:T(8,128)(2,1)S(1)}, bf16[192,512]{1,0:T(8,128)(2,1)S(1)}, u32[]{:S(2)}, u32[]{:S(2)}) collective-permute-start(bf16[192,512]{1,0:T(8,128)(2,1)S(1)} %get-tuple-element.82), channel_id=1, source_target_pairs={{0,1},{1,0},{2,3},{3,2},{4,5},{5,4},{6,7},{7,6},{8,9},{9,8},{10,11... | collective-permute-start | bytes 589832 | tf_op jit(solution)/shard_map/ppermute | solution.py:424
  18.6 8.9 %collective-permute-start.11 = (bf16[192,512]{1,0:T(8,128)(2,1)S(1)}, bf16[192,512]{1,0:T(8,128)(2,1)S(1)}, u32[]{:S(2)}, u32[]{:S(2)}) collective-permute-start(bf16[192,512]{1,0:T(8,128)(2,1)S(1)} %get-tuple-element.88), channel_id=1, source_target_pairs={{0,2},{1,4},{2,0},{3,6},{4,1},{5,8},{6,3},{7,10},{8,5},{9,12},{10,... | collective-permute-start | bytes 589832 | tf_op jit(solution)/shard_map/ppermute | solution.py:425
  20.6 6.3 %collective-permute-start.10 = (f32[5,8,512]{2,1,0:T(8,128)S(1)}, f32[5,8,512]{2,1,0:T(8,128)S(1)}, u32[]{:S(2)}, u32[]{:S(2)}) collective-permute-start(f32[5,8,512]{2,1,0:T(8,128)S(1)} %shard_map.94.refs_4_.refs_9_), channel_id=1, source_target_pairs={{0,2},{1,3},{2,0},{3,1},{4,6},{5,7},{6,4},{7,5},{8,10},{9,11},{10,... | collective-permute-start | bytes 245768 | tf_op jit(solution)/shard_map/ppermute | solution.py:426
  20.9 6.1 %collective-permute-start.9 = (bf16[5,8,512]{2,1,0:T(8,128)(2,1)S(1)}, bf16[5,8,512]{2,1,0:T(8,128)(2,1)S(1)}, u32[]{:S(2)}, u32[]{:S(2)}) collective-permute-start(bf16[5,8,512]{2,1,0:T(8,128)(2,1)S(1)} %get-tuple-element.83.refs_5_), channel_id=1, source_target_pairs={{0,2},{1,3},{2,0},{3,1},{4,6},{5,7},{6,4},{7,5},{8,10},{9,11},{10,... | collective-permute-start | bytes 122888 | tf_op jit(solution)/shard_map/ppermute | solution.py:426
  27.4 2.6 %collective-permute-start.12 = (bf16[192,512]{1,0:T(8,128)(2,1)S(1)}, bf16[192,512]{1,0:T(8,128)(2,1)S(1)}, u32[]{:S(2)}, u32[]{:S(2)}) collective-permute-start(bf16[192,512]{1,0:T(8,128)(2,1)S(1)} %get-tuple-element.91), channel_id=1, source_target_pairs={{0,1},{1,0},{2,3},{3,2},{4,5},{5,4},{6,7},{7,6},{8,9},{9,8},{10,11... | collective-permute-start | bytes 589832 | tf_op jit(solution)/shard_map/ppermute | solution.py:424
  27.9 5.7 %collective-permute-start.13 = (bf16[192,512]{1,0:T(8,128)(2,1)S(1)}, bf16[192,512]{1,0:T(8,128)(2,1)S(1)}, u32[]{:S(2)}, u32[]{:S(2)}) collective-permute-start(bf16[192,512]{1,0:T(8,128)(2,1)S(1)} %get-tuple-element.95), channel_id=1, source_target_pairs={{0,2},{1,4},{2,0},{3,6},{4,1},{5,8},{6,3},{7,10},{8,5},{9,12},{10,... | collective-permute-start | bytes 589832 | tf_op jit(solution)/shard_map/ppermute | solution.py:425
  30.0 9.5 %collective-permute-start.16 = (f32[2,96,512]{2,1,0:T(8,128)S(1)}, f32[2,96,512]{2,1,0:T(8,128)S(1)}, u32[]{:S(2)}, u32[]{:S(2)}) collective-permute-start(f32[2,96,512]{2,1,0:T(8,128)S(1)} %get-tuple-element.102), channel_id=1, source_target_pairs={{0,1},{1,0},{2,3},{3,2},{4,5},{5,4},{6,7},{7,6},{8,9},{9,8},{10,11... | collective-permute-start | bytes 1179656 | tf_op jit(solution)/shard_map/ppermute | solution.py:424
  34.0 5.5 %copy-start.1 = (f32[4,24,2048]{2,1,0:T(8,128)S(1)}, f32[4,24,2048]{2,1,0:T(8,128)}, u32[]{:S(2)}) copy-start(f32[4,24,2048]{2,1,0:T(8,128)} %refs_0_.5) | copy-start | bytes 2359300
  34.1 2.6 %collective-permute-start.15 = (f32[136,512]{1,0:T(8,128)S(1)}, f32[136,512]{1,0:T(8,128)S(1)}, u32[]{:S(2)}, u32[]{:S(2)}) collective-permute-start(f32[136,512]{1,0:T(8,128)S(1)} %get-tuple-element.99), channel_id=1, source_target_pairs={{0,1},{1,0},{2,3},{3,2},{4,5},{5,4},{6,7},{7,6},{8,9},{9,8},{10,11... | collective-permute-start | bytes 835592 | tf_op jit(solution)/shard_map/ppermute | solution.py:424
  34.5 3.7 %collective-permute-start.14 = (f32[136,512]{1,0:T(8,128)S(1)}, f32[136,512]{1,0:T(8,128)S(1)}, u32[]{:S(2)}, u32[]{:S(2)}) collective-permute-start(f32[136,512]{1,0:T(8,128)S(1)} %get-tuple-element.98), channel_id=1, source_target_pairs={{0,1},{1,0},{2,3},{3,2},{4,5},{5,4},{6,7},{7,6},{8,9},{9,8},{10,11... | collective-permute-start | bytes 835592 | tf_op jit(solution)/shard_map/ppermute | solution.py:424
  34.7 4.9 %collective-permute-start.20 = (bf16[5,8,512]{2,1,0:T(8,128)(2,1)S(1)}, bf16[5,8,512]{2,1,0:T(8,128)(2,1)S(1)}, u32[]{:S(2)}, u32[]{:S(2)}) collective-permute-start(bf16[5,8,512]{2,1,0:T(8,128)(2,1)S(1)} %get-tuple-element.97.refs_4_), channel_id=1, source_target_pairs={{0,3},{1,2},{2,1},{3,0},{4,7},{5,6},{6,5},{7,4},{8,11},{9,10},{10,... | collective-permute-start | bytes 122888 | tf_op jit(solution)/shard_map/ppermute | solution.py:426
  36.4 4.3 %collective-permute-start.18 = (bf16[5,8,512]{2,1,0:T(8,128)(2,1)S(1)}, bf16[5,8,512]{2,1,0:T(8,128)(2,1)S(1)}, u32[]{:S(2)}, u32[]{:S(2)}) collective-permute-start(bf16[5,8,512]{2,1,0:T(8,128)(2,1)S(1)} %get-tuple-element.97.refs_4_), channel_id=1, source_target_pairs={{0,2},{1,3},{2,0},{3,1},{4,6},{5,7},{6,4},{7,5},{8,10},{9,11},{10,... | collective-permute-start | bytes 122888 | tf_op jit(solution)/shard_map/ppermute | solution.py:426
  36.7 4.0 %collective-permute-start.19 = (bf16[5,8,512]{2,1,0:T(8,128)(2,1)S(1)}, bf16[5,8,512]{2,1,0:T(8,128)(2,1)S(1)}, u32[]{:S(2)}, u32[]{:S(2)}) collective-permute-start(bf16[5,8,512]{2,1,0:T(8,128)(2,1)S(1)} %get-tuple-element.104), channel_id=1, source_target_pairs={{0,3},{1,2},{2,1},{3,0},{4,7},{5,6},{6,5},{7,4},{8,11},{9,10},{10,... | collective-permute-start | bytes 122888 | tf_op jit(solution)/shard_map/ppermute | solution.py:426
  38.2 4.0 %collective-permute-start.17 = (bf16[5,8,512]{2,1,0:T(8,128)(2,1)S(1)}, bf16[5,8,512]{2,1,0:T(8,128)(2,1)S(1)}, u32[]{:S(2)}, u32[]{:S(2)}) collective-permute-start(bf16[5,8,512]{2,1,0:T(8,128)(2,1)S(1)} %get-tuple-element.104), channel_id=1, source_target_pairs={{0,2},{1,3},{2,0},{3,1},{4,6},{5,7},{6,4},{7,5},{8,10},{9,11},{10,... | collective-permute-start | bytes 122888 | tf_op jit(solution)/shard_map/ppermute | solution.py:426
